TPU v7x, 128 devices: a whole 4x4x4 slice. The times are simulated.
128 devices in a mesh: slab: 4 (over y_lo, core), vel: 32 (over x, y_hi, z).
Axes of the slice: x: 4, y: 4 (y_hi: 2, y_lo: 2; y = y_hi * 2 + y_lo), z: 4, core: 2. Of those that a mesh axis runs over, the one named last changes fastest.
Arguments:
- dist: float32 [24576, 16, 128], P('vel', 'slab'), may hold values from -6 to 6
- speeds: float32 [3, 24576], P(None, 'vel'), may hold values from -4 to 4
- weights: float32 [24576], P('vel'), may hold values from 0.5 to 2
- collision: float32 [16, 128], P('slab'), may hold values from 0.3 to 3
- wall_values: float32 [2, 24576], P(None, 'vel'), may hold values from -6 to 6
- wall_kind: int32 [2, 24576], P(None, 'vel'), may hold values from 0 to 1
Outputs:
- final_dist: float32 [24576, 16, 128], P('vel', 'slab')
- settled: float32 [5, 16, 128], P(None, 'slab')
Inputs may be any that keep to these rules, and one draw needn't show every extreme that they name: `wall_kind`: 1 lets the wall's value enter for velocities leaving that wall, 0 makes the wall absorbing.
All inputs are finite; a program needn't handle non-finite values.
Results may differ from a plain program's by a relative error of at most 0.0003.
Values sent between devices are 32-bit elements; how exact they have to be, the bound alone decides.
A program may use at most 64 MiB of HBM per device.

v0:
```python
import jax
import jax.numpy as jnp
from jax import lax
from jax.sharding import PartitionSpec as P

VELS = 24576
ITERS = 2
JACOBI = 2


PRECISE = lax.Precision.HIGHEST


def from_everyone(shard, axis):
    devices = lax.axis_size(axis)
    return lax.all_to_all(
        jnp.broadcast_to(shard[None], (devices, *shard.shape)), axis, 0, 0, tiled=True
    )


def of_everyone(shard, axis):
    everything = from_everyone(shard, axis)
    return jnp.sum(everything, axis=0)


def extended_2(cells, sides, width):
    for axis, dim in sides:
        count = lax.axis_size(axis)
        ends = count - 1
        head = lax.slice_in_dim(cells, 0, width, axis=dim)
        tail = lax.slice_in_dim(cells, cells.shape[dim] - width, cells.shape[dim], axis=dim)
        cells = jnp.concatenate(
            [
                lax.ppermute(tail, axis, [(i, (i + 1) % count) for i in range(ends)]),
                cells,
                lax.ppermute(head, axis, [((i + 1) % count, i) for i in range(ends)]),
            ],
            axis=dim,
        )
    return cells


def laid_out(parts, dim):
    shape = list(parts.shape[1:])
    shape[dim] *= parts.shape[0]
    return jnp.moveaxis(parts, 0, dim).reshape(shape)


def collect(shard, axis, dim):
    return laid_out(from_everyone(shard, axis), dim)


def moment_rows(speeds):
    speed_x, speed_y, speed_z = (speeds[0], speeds[1], speeds[2])
    square = speed_x * speed_x + speed_y * speed_y + speed_z * speed_z
    third = square / 3.0
    return jnp.stack(
        [
            jnp.ones_like(speed_x),
            speed_x,
            speed_y,
            speed_z,
            2.0 / 3.0 * square - 1.0,
            speed_x * (square - 2.5),
            speed_y * (square - 2.5),
            speed_z * (square - 2.5),
            speed_x * speed_x - third,
            speed_x * speed_y,
            speed_x * speed_z,
            speed_y * speed_y - third,
            speed_y * speed_z,
        ]
    )


def shape_rows(speeds):
    speed_x, speed_y, speed_z = (speeds[0], speeds[1], speeds[2])
    square = speed_x * speed_x + speed_y * speed_y + speed_z * speed_z
    factor = 4.0 / 45.0 * (square - 2.5)
    return jnp.stack(
        [
            jnp.ones_like(speed_x),
            2.0 * speed_x,
            2.0 * speed_y,
            2.0 * speed_z,
            square - 1.5,
            factor * speed_x,
            factor * speed_y,
            factor * speed_z,
        ],
        axis=1,
    )


def macro_fields(moment, collision, widen):
    widened = widen(moment)

    def diff_x(which):
        return 0.5 * (widened[which, 2:, 1:-1] - widened[which, :-2, 1:-1])

    def diff_y(which):
        return 0.5 * (widened[which, 1:-1, 2:] - widened[which, 1:-1, :-2])

    fluxes = jnp.stack(
        [
            -(diff_x(1) + diff_y(2)),
            -(diff_x(8) + diff_y(9)),
            -(diff_x(9) + diff_y(11)),
            -(diff_x(10) + diff_y(12)),
            -(diff_x(5) + diff_y(6)),
        ]
    )
    target = moment[:5] + fluxes
    stiffness = 1.0 / collision
    beside_all = widened[:5]
    settled = moment[:5]
    for jacobi_turn in range(JACOBI):
        if jacobi_turn > 0:
            beside_all = widen(settled)
        neighbours = (
            beside_all[:, 2:, 1:-1]
            + beside_all[:, :-2, 1:-1]
            + beside_all[:, 1:-1, 2:]
            + beside_all[:, 1:-1, :-2]
        )
        settled = (target + stiffness * neighbours) / (1.0 + 4.0 * stiffness)
    return settled


def combine(earlier, later):
    return (earlier[0] * later[0], later[0] * earlier[1] + later[1])


def sweep_across(factor, source, axis):
    return lax.associative_scan(combine, (factor, source), axis=axis)


def along_y(values, speed_y):
    cross_rate = (jnp.abs(speed_y) * values.shape[2])[:, None, None]
    forward = (speed_y >= 0)[:, None, None]
    factor = jnp.broadcast_to(cross_rate / (1.0 + cross_rate), values.shape)
    source = values / (1.0 + cross_rate)
    source = jnp.where(forward, source, source[:, :, ::-1])
    result = sweep_across(factor, source, 2)[1]
    return jnp.where(forward, result, result[:, :, ::-1])


def upwind_terms(values, equilibrium, speed_x, collision, cells):
    cross_rate = (jnp.abs(speed_x) * cells)[:, None, None]
    denominator = 1.0 + cross_rate + collision[None]
    factor = cross_rate / denominator
    source = (values + collision[None] * equilibrium) / denominator
    forward = (speed_x >= 0)[:, None, None]
    factor = jnp.where(forward, factor, factor[:, ::-1, :])
    source = jnp.where(forward, source, source[:, ::-1, :])
    return (factor, source, forward)


def link_slabs(slab_factors, slab_sources, members, position, identity):
    from_lower = identity
    from_upper = identity
    for member in range(members):
        joined = combine(from_lower, (slab_factors(member), slab_sources(member)))
        taken = member < position
        from_lower = (
            jnp.where(taken, joined[0], from_lower[0]),
            jnp.where(taken, joined[1], from_lower[1]),
        )
    for member in reversed(range(members)):
        joined = combine(from_upper, (slab_factors(member), slab_sources(member)))
        taken = member > position
        from_upper = (
            jnp.where(taken, joined[0], from_upper[0]),
            jnp.where(taken, joined[1], from_upper[1]),
        )
    return (from_lower, from_upper)


def on_device(dist, speeds, weights, collision, wall_values, wall_kind):
    inflow = wall_values * wall_kind.astype(jnp.float32)
    rows = moment_rows(speeds) * weights[None] / VELS
    shapes = shape_rows(speeds)
    members = lax.axis_size("slab")
    cells = dist.shape[1] * members
    position = lax.axis_index("slab")
    count_vel = dist.shape[0]
    every_rate = lax.all_gather(collision, "slab", axis=0, tiled=True)
    cross_all = (jnp.abs(speeds[0]) * cells)[:, None, None]
    cell_factor = cross_all / (1.0 + cross_all + every_rate[None])
    slab_products = jnp.prod(
        cell_factor.reshape(count_vel, members, dist.shape[1], dist.shape[2]), axis=2
    )
    field = dist
    settled = jnp.zeros((5, dist.shape[1], dist.shape[2]), jnp.float32)
    for outer_turn in range(ITERS):
        partial_sum = jnp.einsum("kv,vxy->kxy", rows, field, precision=PRECISE)
        moment = of_everyone(partial_sum, "vel")

        def widen_slab(values):
            extended = extended_2(values, (("slab", 1),), 1)
            return jnp.pad(extended, ((0, 0), (0, 0), (1, 1)))

        settled = macro_fields(moment, collision, widen_slab)
        drive = jnp.concatenate([settled, moment[5:8]], 0)
        equilibrium = jnp.einsum("vk,kxy->vxy", shapes, drive, precision=PRECISE)
        factor, source, forward = upwind_terms(field, equilibrium, speeds[0], collision, cells)
        product, accrued = sweep_across(factor, source, 1)
        end_maps = (product[:, -1, :], accrued[:, -1, :])
        identity = (jnp.ones_like(end_maps[0]), jnp.zeros_like(end_maps[1]))
        every_source = collect(end_maps[1], "slab", 0)
        all_sources = every_source.reshape(members, count_vel, -1)
        from_lower, from_upper = link_slabs(
            lambda member: slab_products[:, member],
            lambda member: all_sources[member],
            members,
            position,
            identity,
        )
        enter_low = from_lower[0] * inflow[0][:, None] + from_lower[1]
        enter_high = from_upper[0] * inflow[1][:, None] + from_upper[1]
        entering = jnp.where((speeds[0] >= 0)[:, None], enter_low, enter_high)
        flipped = product * entering[:, None, :] + accrued
        inner = jnp.where(forward, flipped, flipped[:, ::-1, :])
        field = along_y(inner, speeds[1])
    return (field, settled)


def solution(mesh):
    return jax.shard_map(
        on_device,
        mesh=mesh,
        in_specs=(
            P("vel", "slab", None),
            P(None, "vel"),
            P("vel"),
            P("slab", None),
            P(None, "vel"),
            P(None, "vel"),
        ),
        out_specs=(P("vel", "slab", None), P(None, "slab", None)),
        check_vma=False,
    )
```

profile of v0, /device:TPU:1, one launch (start us, length us, event | category | flops | bytes accessed | tf_op | source)
XLA Modules:
  0.0 334.7 jit_solution(1046896258087386955)
XLA Ops:
  2.1 1.7 copy.57
  6.4 11.3 %all-to-all-start = ((f32[32,13,4,128]{3,2,1,0:T(4,128)}), f32[32,13,4,128]{3,2,1,0:T(4,128)S(1)}, u32[]{:S(2)}, u32[]{:S(2)}) async-start(f32[32,13,4,128]{3,2,1,0:T(4,128)} %broadcast_in_dim.110), calls=%async_computation | async-start | bytes 1703936 | tf_op jit(solution)/shard_map/all_to_all | solution.py:16
  18.5 13.2 %all-to-all-done = f32[32,13,4,128]{3,2,1,0:T(4,128)S(1)} async-done(((f32[32,13,4,128]{3,2,1,0:T(4,128)}), f32[32,13,4,128]{3,2,1,0:T(4,128)S(1)}, u32[]{:S(2)}, u32[]{:S(2)}) %all-to-all-start) | async-done | bytes 852000 | tf_op jit(solution)/shard_map/all_to_all | solution.py:16
  31.9 5.2 %collective-permute-start.1 = (f32[13,1,128]{2,0,1:T(8,128)S(1)}, f32[13,1,128]{2,0,1:T(8,128)S(1)}, u32[]{:S(2)}, u32[]{:S(2)}) collective-permute-start(f32[13,1,128]{2,0,1:T(8,128)S(1)} %get-tuple-element.52), channel_id=1, source_target_pairs={{0,32},{32,64},{64,96},{1,33},{33,65},{65,97},{2,34},{34,66},{66,9... | collective-permute-start | bytes 19976 | tf_op jit(solution)/shard_map/ppermute | solution.py:34
  37.8 1.9 collective-permute-start
  39.8 3.0 collective-permute-done
  43.2 1.9 collective-permute-start.2
  45.1 3.6 %collective-permute-start.3 = (f32[5,1,128]{2,0,1:T(8,128)S(1)}, f32[5,1,128]{2,0,1:T(8,128)S(1)}, u32[]{:S(2)}, u32[]{:S(2)}) collective-permute-start(f32[5,1,128]{2,0,1:T(8,128)S(1)} %get-tuple-element.64), channel_id=1, source_target_pairs={{0,32},{32,64},{64,96},{1,33},{33,65},{65,97},{2,34},{34,66},{66,9... | collective-permute-start | bytes 7688 | tf_op jit(solution)/shard_map/ppermute | solution.py:34
  48.8 4.5 %all-gather = f32[4,4,128]{2,1,0:T(4,128)} all-gather(f32[1,4,128]{2,1,0:T(4,128)S(1)} %bitcast.82), channel_id=1, replica_groups=mesh['slab'=4,'vel'=32] {'slab'}, dimensions={0}, use_global_device_ids=true | all-gather | bytes 10240 | tf_op jit(solution)/shard_map/all_gather | solution.py:187
  61.1 3.1 pad.152
  64.2 1.8 add_bitcast_fusion.1
  66.0 1.9 copy.58
  67.9 2.2 broadcast_in_dim.112
  70.1 4.8 %all-to-all-start.1 = ((f32[4,768,128]{2,1,0:T(8,128)}), f32[4,768,128]{2,1,0:T(8,128)}, u32[]{:S(2)}, u32[]{:S(2)}) async-start(f32[4,768,128]{2,1,0:T(8,128)} %broadcast_in_dim.112), calls=%async_computation.1 | async-start | bytes 3145728 | tf_op jit(solution)/shard_map/all_to_all | solution.py:16
  75.6 1.8 divide_reduce_fusion
  78.5 3.2 pad.145
  81.6 1.9 pad_add_fusion.2
  83.6 3.1 pad.146
  86.7 7.4 %all-to-all-done.1 = f32[4,768,128]{2,1,0:T(8,128)} async-done(((f32[4,768,128]{2,1,0:T(8,128)}), f32[4,768,128]{2,1,0:T(8,128)}, u32[]{:S(2)}, u32[]{:S(2)}) %all-to-all-start.1) | async-done | bytes 1572896 | tf_op jit(solution)/shard_map/all_to_all | solution.py:16
  94.1 2.8 select_bitcast_fusion.1
  98.1 4.4 %multiply_add_fusion.1 = (f32[768,4,128]{0,2,1:T(8,128)S(1)}, f32[768,4,128]{0,2,1:T(8,128)}) fusion(f32[768,4,128]{0,2,1:T(8,128)} %copy-done.4, f32[768,4,128]{0,2,1:T(8,128)} %pad.152, f32[768,128]{0,1:T(8,128)S(1)} %copy.59, f32[768,4,128]{0,2,1:T(8,128)} %pad.145, f32[768,4,128]{0,2,1:T(8,128)} %pad.146), kind=kLoop, calls=%fused_computation.12 | loop fusion | flops 1572864 | bytes 9830400 | tf_op jit(solution)/shard_map/add | solution.py:222
  103.8 12.8 %rev.31 = f32[768,4,128]{0,2,1:T(8,128)} reverse(f32[768,4,128]{0,2,1:T(8,128)} %fusion), dimensions={2} | reverse | bytes 3145728 | tf_op jit(solution)/shard_map/rev | solution.py:143
  116.6 2.8 broadcast_select_fusion.3
  119.4 3.6 %slice.813 = f32[768,4,63]{0,2,1:T(8,128)} slice(f32[768,4,128]{0,2,1:T(8,128)} %broadcast_select_fusion.3), slice={[0:768:1], [0:4:1], [2:128:2]} | slice | bytes 1548288 | tf_op jit(solution)/shard_map/slice | solution.py:135
  126.2 2.3 multiply_add_fusion.3
  128.6 1.8 slice.778
  130.4 1.8 slice.777
  135.6 1.7 multiply_add_fusion.7
  169.3 2.0 pad.164
  174.4 2.9 pad.165
  177.3 3.0 pad.166
  180.3 2.1 add.665
  182.4 7.8 %rev.32 = f32[768,4,128]{0,2,1:T(8,128)} reverse(f32[768,4,128]{0,2,1:T(8,128)S(1)} %add.665), dimensions={2} | reverse | bytes 3145728 | tf_op jit(solution)/shard_map/rev | solution.py:145
  190.2 2.8 fusion.4
  193.2 18.3 %all_to_all.20 = f32[32,13,4,128]{3,2,1,0:T(4,128)} all-to-all(f32[32,13,4,128]{3,2,1,0:T(4,128)S(1)} %broadcast_in_dim.113), channel_id=1, replica_groups=mesh['slab'=4,'vel'=32] {'vel'}, dimensions={0} | all-to-all | bytes 1703936 | tf_op jit(solution)/shard_map/all_to_all | solution.py:16
  212.8 5.0 %collective-permute-start.5 = (f32[13,1,128]{2,0,1:T(8,128)S(1)}, f32[13,1,128]{2,0,1:T(8,128)S(1)}, u32[]{:S(2)}, u32[]{:S(2)}) collective-permute-start(f32[13,1,128]{2,0,1:T(8,128)S(1)} %get-tuple-element.50), channel_id=1, source_target_pairs={{0,32},{32,64},{64,96},{1,33},{33,65},{65,97},{2,34},{34,66},{66,9... | collective-permute-start | bytes 19976 | tf_op jit(solution)/shard_map/ppermute | solution.py:34
  217.8 1.9 collective-permute-start.4
  219.7 3.0 collective-permute-done.4
  223.2 2.0 collective-permute-start.6
  225.2 3.6 %collective-permute-start.7 = (f32[5,1,128]{2,0,1:T(8,128)S(1)}, f32[5,1,128]{2,0,1:T(8,128)S(1)}, u32[]{:S(2)}, u32[]{:S(2)}) collective-permute-start(f32[5,1,128]{2,0,1:T(8,128)S(1)} %get-tuple-element.62), channel_id=1, source_target_pairs={{0,32},{32,64},{64,96},{1,33},{33,65},{65,97},{2,34},{34,66},{66,9... | collective-permute-start | bytes 7688 | tf_op jit(solution)/shard_map/ppermute | solution.py:34
  237.5 2.2 broadcast_in_dim.115
  239.7 4.1 %all-to-all-start.3 = ((f32[4,768,128]{2,1,0:T(8,128)}), f32[4,768,128]{2,1,0:T(8,128)S(1)}, u32[]{:S(2)}, u32[]{:S(2)}) async-start(f32[4,768,128]{2,1,0:T(8,128)} %broadcast_in_dim.115), calls=%async_computation.3 | async-start | bytes 3145728 | tf_op jit(solution)/shard_map/all_to_all | solution.py:16
  244.4 18.0 %all-to-all-done.3 = f32[4,768,128]{2,1,0:T(8,128)S(1)} async-done(((f32[4,768,128]{2,1,0:T(8,128)}), f32[4,768,128]{2,1,0:T(8,128)S(1)}, u32[]{:S(2)}, u32[]{:S(2)}) %all-to-all-start.3) | async-done | bytes 1572896 | tf_op jit(solution)/shard_map/all_to_all | solution.py:16
  264.2 2.7 multiply_add_fusion
  267.0 7.7 %rev.35 = f32[768,4,128]{0,2,1:T(8,128)} reverse(f32[768,4,128]{0,2,1:T(8,128)S(1)} %fusion.1), dimensions={2} | reverse | bytes 3145728 | tf_op jit(solution)/shard_map/rev | solution.py:143
  286.6 1.7 multiply_add_fusion.6
  319.4 2.9 pad.186
  323.8 7.7 %rev.36 = f32[768,4,128]{0,2,1:T(8,128)} reverse(f32[768,4,128]{0,2,1:T(8,128)S(1)} %add.716), dimensions={2} | reverse | bytes 3145728 | tf_op jit(solution)/shard_map/rev | solution.py:145
  (345 shorter events, 119.4 us)
Async XLA Ops:
  2.1 52.9 %copy-start.46 = (f32[768]{0:T(1024)}, f32[768]{0:T(1024)S(1)}, u32[]{:S(2)}) copy-start(f32[768]{0:T(1024)S(1)} %get-tuple-element.13) | copy-start | bytes 9220
  5.4 12.4 %copy-start.67 = (f32[4,128]{1,0:T(4,128)S(1)}, f32[4,128]{1,0:T(4,128)}, u32[]{:S(2)}) copy-start(f32[4,128]{1,0:T(4,128)} %param.9) | copy-start | bytes 6148
  5.4 13.1 %copy-start.72 = (f32[2,768]{1,0:T(2,128)S(1)}, f32[2,768]{1,0:T(2,128)}, u32[]{:S(2)}) copy-start(f32[2,768]{1,0:T(2,128)} %param.10) | copy-start | bytes 18436
  5.4 13.1 %copy-start.73 = (s32[2,768]{1,0:T(2,128)S(1)}, s32[2,768]{1,0:T(2,128)}, u32[]{:S(2)}) copy-start(s32[2,768]{1,0:T(2,128)} %param.11) | copy-start | bytes 18436
  6.4 25.4 %all-to-all-start = ((f32[32,13,4,128]{3,2,1,0:T(4,128)}), f32[32,13,4,128]{3,2,1,0:T(4,128)S(1)}, u32[]{:S(2)}, u32[]{:S(2)}) async-start(f32[32,13,4,128]{3,2,1,0:T(4,128)} %broadcast_in_dim.110), calls=%async_computation | async-start | bytes 1703936 | tf_op jit(solution)/shard_map/all_to_all | solution.py:16
  17.8 37.1 %copy-start.47 = (f32[768]{0:T(1024)}, f32[768]{0:T(1024)S(1)}, u32[]{:S(2)}) copy-start(f32[768]{0:T(1024)S(1)} %broadcast_add_fusion.1) | copy-start | bytes 9220
  17.8 37.1 %copy-start.49 = (f32[4,128]{1,0:T(4,128)}, f32[4,128]{1,0:T(4,128)S(1)}, u32[]{:S(2)}) copy-start(f32[4,128]{1,0:T(4,128)S(1)} %get-tuple-element.18) | copy-start | bytes 6148
  17.8 37.1 %copy-start.51 = (f32[4,128]{1,0:T(4,128)}, f32[4,128]{1,0:T(4,128)S(1)}, u32[]{:S(2)}) copy-start(f32[4,128]{1,0:T(4,128)S(1)} %get-tuple-element.19) | copy-start | bytes 6148
  18.5 36.9 %copy-start.40 = (pred[768]{0:T(1024)(128)(4,1)}, pred[768]{0:T(1024)(128)(4,1)S(1)}, u32[]{:S(2)}) copy-start(pred[768]{0:T(1024)(128)(4,1)S(1)} %get-tuple-element.11) | copy-start | bytes 2308
  31.9 7.8 %collective-permute-start.1 = (f32[13,1,128]{2,0,1:T(8,128)S(1)}, f32[13,1,128]{2,0,1:T(8,128)S(1)}, u32[]{:S(2)}, u32[]{:S(2)}) collective-permute-start(f32[13,1,128]{2,0,1:T(8,128)S(1)} %get-tuple-element.52), channel_id=1, source_target_pairs={{0,32},{32,64},{64,96},{1,33},{33,65},{65,97},{2,34},{34,66},{66,9... | collective-permute-start | bytes 19976 | tf_op jit(solution)/shard_map/ppermute | solution.py:34
  37.8 17.6 %copy-start.22 = (f32[768,8]{0,1:T(8,128)}, f32[768,8]{0,1:T(8,128)S(1)}, u32[]{:S(2)}) copy-start(f32[768,8]{0,1:T(8,128)S(1)} %stack.9) | copy-start | bytes 73732
  37.8 5.0 %collective-permute-start = (f32[13,1,128]{2,0,1:T(8,128)S(1)}, f32[13,1,128]{2,0,1:T(8,128)S(1)}, u32[]{:S(2)}, u32[]{:S(2)}) collective-permute-start(f32[13,1,128]{2,0,1:T(8,128)S(1)} %get-tuple-element.53), channel_id=1, source_target_pairs={{32,0},{64,32},{96,64},{33,1},{65,33},{97,65},{34,2},{66,34},{98,6... | collective-permute-start | bytes 19976 | tf_op jit(solution)/shard_map/ppermute | solution.py:36
  43.2 10.1 %collective-permute-start.2 = (f32[5,1,128]{2,0,1:T(8,128)S(1)}, f32[5,1,128]{2,0,1:T(8,128)S(1)}, u32[]{:S(2)}, u32[]{:S(2)}) collective-permute-start(f32[5,1,128]{2,0,1:T(8,128)S(1)} %get-tuple-element.65), channel_id=1, source_target_pairs={{32,0},{64,32},{96,64},{33,1},{65,33},{97,65},{34,2},{66,34},{98,6... | collective-permute-start | bytes 7688 | tf_op jit(solution)/shard_map/ppermute | solution.py:36
  45.1 8.1 %collective-permute-start.3 = (f32[5,1,128]{2,0,1:T(8,128)S(1)}, f32[5,1,128]{2,0,1:T(8,128)S(1)}, u32[]{:S(2)}, u32[]{:S(2)}) collective-permute-start(f32[5,1,128]{2,0,1:T(8,128)S(1)} %get-tuple-element.64), channel_id=1, source_target_pairs={{0,32},{32,64},{64,96},{1,33},{33,65},{65,97},{2,34},{34,66},{66,9... | collective-permute-start | bytes 7688 | tf_op jit(solution)/shard_map/ppermute | solution.py:34
  70.1 24.0 %all-to-all-start.1 = ((f32[4,768,128]{2,1,0:T(8,128)}), f32[4,768,128]{2,1,0:T(8,128)}, u32[]{:S(2)}, u32[]{:S(2)}) async-start(f32[4,768,128]{2,1,0:T(8,128)} %broadcast_in_dim.112), calls=%async_computation.1 | async-start | bytes 3145728 | tf_op jit(solution)/shard_map/all_to_all | solution.py:16
  75.5 56.7 %copy-start.26 = (f32[768]{0:T(1024)}, f32[768]{0:T(1024)S(1)}, u32[]{:S(2)}) copy-start(f32[768]{0:T(1024)S(1)} %get-tuple-element.83) | copy-start | bytes 9220
  75.5 60.0 %copy-start.30 = (f32[768]{0:T(1024)}, f32[768]{0:T(1024)S(1)}, u32[]{:S(2)}) copy-start(f32[768]{0:T(1024)S(1)} %get-tuple-element.84) | copy-start | bytes 9220
  75.5 64.9 %copy-start.34 = (f32[768]{0:T(1024)}, f32[768]{0:T(1024)S(1)}, u32[]{:S(2)}) copy-start(f32[768]{0:T(1024)S(1)} %get-tuple-element.86) | copy-start | bytes 9220
  75.5 97.7 %copy-start.24 = (f32[768]{0:T(1024)}, f32[768]{0:T(1024)S(1)}, u32[]{:S(2)}) copy-start(f32[768]{0:T(1024)S(1)} %get-tuple-element.88) | copy-start | bytes 9220
  77.4 16.7 %copy-start = (f32[768,4,128]{2,0,1:T(8,128)}, f32[768,4,128]{2,0,1:T(8,128)S(1)}, u32[]{:S(2)}) copy-start(f32[768,4,128]{2,0,1:T(8,128)S(1)} %divide_reduce_fusion) | copy-start | bytes 4718596
  83.6 10.5 %copy-start.41 = (pred[768]{0:T(1024)(128)(4,1)S(1)}, pred[768]{0:T(1024)(128)(4,1)}, u32[]{:S(2)}) copy-start(pred[768]{0:T(1024)(128)(4,1)} %copy-done.40) | copy-start | bytes 2308
  83.6 10.5 %copy-start.61 = (f32[768]{0:T(1024)S(1)}, f32[768]{0:T(1024)}, u32[]{:S(2)}) copy-start(f32[768]{0:T(1024)} %get-tuple-element.14) | copy-start | bytes 9220
  83.6 10.5 %copy-start.62 = (f32[768]{0:T(1024)S(1)}, f32[768]{0:T(1024)}, u32[]{:S(2)}) copy-start(f32[768]{0:T(1024)} %get-tuple-element.15) | copy-start | bytes 9220
  103.8 12.8 %copy-start.38 = (f32[768]{0:T(1024)S(1)}, f32[768]{0:T(1024)}, u32[]{:S(2)}) copy-start(f32[768]{0:T(1024)} %get-tuple-element.89) | copy-start | bytes 9220
  103.8 12.8 %copy-start.43 = (pred[768]{0:T(1024)(128)(4,1)S(1)}, pred[768]{0:T(1024)(128)(4,1)}, u32[]{:S(2)}) copy-start(pred[768]{0:T(1024)(128)(4,1)} %copy-done.40) | copy-start | bytes 2308
  103.8 12.8 %copy-start.63 = (pred[768]{0:T(1024)(128)(4,1)S(1)}, pred[768]{0:T(1024)(128)(4,1)}, u32[]{:S(2)}) copy-start(pred[768]{0:T(1024)(128)(4,1)} %get-tuple-element.10) | copy-start | bytes 2308
  142.1 22.8 %slice-start.1 = ((f32[768,4,8]{0,2,1:T(8,128)}), f32[768,4,1]{0,2,1:T(1,128)S(1)}, s32[]{:S(2)}) async-start(f32[768,4,8]{0,2,1:T(8,128)} %multiply_add_fusion.9), calls=%async_computation.5 | async-start | bytes 24576 | tf_op jit(solution)/shard_map/slice | solution.py:135
  161.6 5.0 %copy-start.16 = (f32[768,4,15]{0,2,1:T(8,128)S(1)}, f32[768,4,15]{0,2,1:T(8,128)}, u32[]{:S(2)}) copy-start(f32[768,4,15]{0,2,1:T(8,128)} %slice.809) | copy-start | bytes 552964
  161.6 5.0 %copy-start.31 = (f32[768]{0:T(1024)S(1)}, f32[768]{0:T(1024)}, u32[]{:S(2)}) copy-start(f32[768]{0:T(1024)} %copy-done.30) | copy-start | bytes 9220
  182.4 7.9 %copy-start.18 = (f32[13,768]{1,0:T(8,128)S(1)}, f32[13,768]{1,0:T(8,128)}, u32[]{:S(2)}) copy-start(f32[13,768]{1,0:T(8,128)} %copy-done.17) | copy-start | bytes 119812
  182.4 7.8 %copy-start.64 = (pred[768]{0:T(1024)(128)(4,1)S(1)}, pred[768]{0:T(1024)(128)(4,1)}, u32[]{:S(2)}) copy-start(pred[768]{0:T(1024)(128)(4,1)} %get-tuple-element.10) | copy-start | bytes 2308
  182.4 7.8 %copy-start.70 = (f32[768]{0:T(1024)S(1)}, f32[768]{0:T(1024)}, u32[]{:S(2)}) copy-start(f32[768]{0:T(1024)} %param.8) | copy-start | bytes 9220
  193.2 29.9 %copy-start.50 = (f32[4,128]{1,0:T(4,128)S(1)}, f32[4,128]{1,0:T(4,128)}, u32[]{:S(2)}) copy-start(f32[4,128]{1,0:T(4,128)} %copy-done.49) | copy-start | bytes 6148
  193.2 29.9 %copy-start.52 = (f32[4,128]{1,0:T(4,128)S(1)}, f32[4,128]{1,0:T(4,128)}, u32[]{:S(2)}) copy-start(f32[4,128]{1,0:T(4,128)} %copy-done.51) | copy-start | bytes 6148
  193.2 36.6 %copy-start.23 = (f32[768,8]{0,1:T(8,128)S(1)}, f32[768,8]{0,1:T(8,128)}, u32[]{:S(2)}) copy-start(f32[768,8]{0,1:T(8,128)} %copy-done.22) | copy-start | bytes 73732
  211.5 19.8 %copy-start.48 = (f32[768]{0:T(1024)S(1)}, f32[768]{0:T(1024)}, u32[]{:S(2)}) copy-start(f32[768]{0:T(1024)} %copy-done.47) | copy-start | bytes 9220
  211.5 19.8 %copy-start.68 = (f32[4,128]{1,0:T(4,128)S(1)}, f32[4,128]{1,0:T(4,128)}, u32[]{:S(2)}) copy-start(f32[4,128]{1,0:T(4,128)} %param.9) | copy-start | bytes 6148
  212.8 6.9 %collective-permute-start.5 = (f32[13,1,128]{2,0,1:T(8,128)S(1)}, f32[13,1,128]{2,0,1:T(8,128)S(1)}, u32[]{:S(2)}, u32[]{:S(2)}) collective-permute-start(f32[13,1,128]{2,0,1:T(8,128)S(1)} %get-tuple-element.50), channel_id=1, source_target_pairs={{0,32},{32,64},{64,96},{1,33},{33,65},{65,97},{2,34},{34,66},{66,9... | collective-permute-start | bytes 19976 | tf_op jit(solution)/shard_map/ppermute | solution.py:34
  217.8 5.0 %collective-permute-start.4 = (f32[13,1,128]{2,0,1:T(8,128)S(1)}, f32[13,1,128]{2,0,1:T(8,128)S(1)}, u32[]{:S(2)}, u32[]{:S(2)}) collective-permute-start(f32[13,1,128]{2,0,1:T(8,128)S(1)} %get-tuple-element.51), channel_id=1, source_target_pairs={{32,0},{64,32},{96,64},{33,1},{65,33},{97,65},{34,2},{66,34},{98,6... | collective-permute-start | bytes 19976 | tf_op jit(solution)/shard_map/ppermute | solution.py:36
  223.1 8.2 %copy-start.2 = (f32[768,4,128]{0,2,1:T(8,128)S(1)}, f32[768,4,128]{0,2,1:T(8,128)}, u32[]{:S(2)}) copy-start(f32[768,4,128]{0,2,1:T(8,128)} %rev.32) | copy-start | bytes 4718596
  223.2 5.7 %collective-permute-start.6 = (f32[5,1,128]{2,0,1:T(8,128)S(1)}, f32[5,1,128]{2,0,1:T(8,128)S(1)}, u32[]{:S(2)}, u32[]{:S(2)}) collective-permute-start(f32[5,1,128]{2,0,1:T(8,128)S(1)} %get-tuple-element.63), channel_id=1, source_target_pairs={{32,0},{64,32},{96,64},{33,1},{65,33},{97,65},{34,2},{66,34},{98,6... | collective-permute-start | bytes 7688 | tf_op jit(solution)/shard_map/ppermute | solution.py:36
  225.2 4.4 %collective-permute-start.7 = (f32[5,1,128]{2,0,1:T(8,128)S(1)}, f32[5,1,128]{2,0,1:T(8,128)S(1)}, u32[]{:S(2)}, u32[]{:S(2)}) collective-permute-start(f32[5,1,128]{2,0,1:T(8,128)S(1)} %get-tuple-element.62), channel_id=1, source_target_pairs={{0,32},{32,64},{64,96},{1,33},{33,65},{65,97},{2,34},{34,66},{66,9... | collective-permute-start | bytes 7688 | tf_op jit(solution)/shard_map/ppermute | solution.py:34
  239.7 22.7 %copy-start.1 = (f32[768,4,128]{2,0,1:T(8,128)S(1)}, f32[768,4,128]{2,0,1:T(8,128)}, u32[]{:S(2)}) copy-start(f32[768,4,128]{2,0,1:T(8,128)} %copy-done) | copy-start | bytes 4718596
  239.7 22.7 %all-to-all-start.3 = ((f32[4,768,128]{2,1,0:T(8,128)}), f32[4,768,128]{2,1,0:T(8,128)S(1)}, u32[]{:S(2)}, u32[]{:S(2)}) async-start(f32[4,768,128]{2,1,0:T(8,128)} %broadcast_in_dim.115), calls=%async_computation.3 | async-start | bytes 3145728 | tf_op jit(solution)/shard_map/all_to_all | solution.py:16
  267.0 7.7 %copy-start.65 = (pred[768]{0:T(1024)(128)(4,1)S(1)}, pred[768]{0:T(1024)(128)(4,1)}, u32[]{:S(2)}) copy-start(pred[768]{0:T(1024)(128)(4,1)} %get-tuple-element.10) | copy-start | bytes 2308
  283.2 8.3 %copy-start.35 = (f32[768]{0:T(1024)S(1)}, f32[768]{0:T(1024)}, u32[]{:S(2)}) copy-start(f32[768]{0:T(1024)} %copy-done.34) | copy-start | bytes 9220
  293.1 20.9 %slice-start = ((f32[768,4,8]{0,2,1:T(8,128)}), f32[768,4,1]{0,2,1:T(1,128)S(1)}, s32[]{:S(2)}) async-start(f32[768,4,8]{0,2,1:T(8,128)} %multiply_add_fusion.8), calls=%async_computation.4 | async-start | bytes 24576 | tf_op jit(solution)/shard_map/slice | solution.py:135
  323.8 7.7 %copy-start.66 = (pred[768]{0:T(1024)(128)(4,1)S(1)}, pred[768]{0:T(1024)(128)(4,1)}, u32[]{:S(2)}) copy-start(pred[768]{0:T(1024)(128)(4,1)} %get-tuple-element.10) | copy-start | bytes 2308
  (39 other events, 103.2 us)
where the time goes:
time: 339 us; the launch traced here: 335 us
  local copies, waits for them, and re-layouts  140 us (41%)
  other arithmetic  71.5 us (21%)
  starting transfers between devices  45.4 us (13%)
  waiting for transfers between devices  45.4 us (13%)
  blocking collectives  22.7 us (7%)
  matrix products  7.11 us (2%)
    slice x46, local copies, waits for them, and re-layouts, sweep_across(): return lax.associative_scan(combine, (factor, source), axis=axis)  53.6 us
    all_to_all x3, waiting for transfers between devices, from_everyone(): lax.all_to_all(jnp.broadcast_to(shard[None], (devices, *shard.shape)), ax...  38.6 us
    pad x30, local copies, waits for them, and re-layouts, sweep_across(): return lax.associative_scan(combine, (factor, source), axis=axis)  29.6 us
    add x25, other arithmetic, combine(): return (earlier[0] * later[0], later[0] * earlier[1] + later[1])  21.6 us
    rev x2, local copies, waits for them, and re-layouts, along_y(): source = jnp.where(forward, source, source[:, :, ::-1])  20.5 us
    all_to_all x3, starting transfers between devices, from_everyone(): lax.all_to_all(jnp.broadcast_to(shard[None], (devices, *shard.shape)), ax...  20.2 us
    all_to_all x1, blocking collectives, from_everyone(): lax.all_to_all(jnp.broadcast_to(shard[None], (devices, *shard.shape)), ax...  18.3 us
    ppermute x4, starting transfers between devices, extended_2(): lax.ppermute(tail, axis, [(i, (i + 1) % count) for i in range(ends)])  17.5 us
  transfers between devices with their start and end apart: 11, of which 6 were waited for; matrix products, arithmetic and copies ran while one was open for 4% of the time, Pallas kernels for 0%

commit v1 on v0

v1 whole, which is shorter than its diff:
```python
import jax
import jax.numpy as jnp
from jax import lax
from jax.experimental import pallas as pl
from jax.experimental.pallas import tpu as pltpu
from jax.sharding import PartitionSpec as P

VELS = 24576
ITERS = 2
JACOBI = 2
NX = 16
NY = 128
SLABS = 4
XL = NX // SLABS
V = VELS // 32
VB = 128
NB = V // VB
PAD = NX - XL
KR = 16
HALF = XL * NY // 2
STEPS = (1, 2, 4, 8, 16, 32, 64)

f32 = jnp.float32
bf16 = jnp.bfloat16
MESH = pl.DeviceIdType.MESH


def split(value):
    high = value.astype(bf16)
    return high, (value - high.astype(f32)).astype(bf16)


def dot(a, b):
    return jnp.dot(a, b, preferred_element_type=f32)


def lanes(shape):
    return lax.broadcasted_iota(jnp.int32, shape, 1)


def mirrored(value):
    return jnp.take_along_axis(value, NY - 1 - lanes(value.shape), axis=1)


def transport_kernel(
    dist, speeds, weights, collision, wall_values, wall_kind,
    out, settled_out,
    draw, gd, fhi, flo, fac, wgt, inv_own, prod, ycoef, ascale, bscale, fxs, fys,
    near, far, outa, outb, rows_t, rows_p, rows_g, shp, col,
    b1, b2, b3, cbuf, crow, dpad, rhs, drive_s,
    dsem, osem, bsend, brecv, ysend, yrecv, csend, crecv, nsend, nrecv, fsend, frecv,
):
    slab = lax.axis_index("slab")
    vel = lax.axis_index("vel")
    px = vel // 8
    py = (vel // 4) % 2
    pz = vel % 4
    edge = jnp.logical_or(slab == 0, slab == SLABS - 1)
    middle = jnp.logical_and(slab > 0, slab < SLABS - 1)
    low_side = slab < 2
    partner = jnp.where(low_side, 1 - slab, 5 - slab)
    across = 3 - slab

    def device(s, x, y, z):
        return {"slab": s, "vel": (x * 2 + y) * 4 + z}

    loads = [
        pltpu.make_async_copy(dist.at[:, x, :], draw.at[x], dsem.at[x]) for x in range(XL)
    ]
    for load in loads:
        load.start()

    peers = []
    for d in range(1, 4):
        peers.append(device(slab, (px + d) % 4, py, pz))
    for d in range(1, 4):
        peers.append(device(slab, px, py, (pz + d) % 4))
    group = py * 4 + slab
    yz = []
    for d in range(1, 8):
        other = (group + d) % 8
        yz.append(device(other % 4, px, other // 4, pz))
    barrier = pltpu.get_barrier_semaphore()
    for peer in peers + yz:
        pl.semaphore_signal(barrier, inc=1, device_id=peer, device_id_type=MESH)

    cx, cy, cz = speeds[0:1, :], speeds[1:2, :], speeds[2:3, :]
    wt = weights[0:1, :]
    square = cx * cx + cy * cy + cz * cz
    third = square / 3.0
    heat = square - 2.5
    one = jnp.ones_like(cx)
    zero = jnp.zeros_like(cx)
    phi = [
        one, cx, cy, cz, 2.0 / 3.0 * square - 1.0, cx * heat, cy * heat, cz * heat,
        cx, cx * cx - third, cx * cy, cx * cz, cx * heat, cy * cy - third, cy * cz, zero,
    ]
    scale = wt / VELS
    fx = jnp.where(cx >= 0, 1.0, 0.0)
    fy = jnp.where(cy >= 0, 1.0, 0.0)
    rows = jnp.concatenate([p * scale for p in phi], axis=0)
    rows_hi, rows_lo = split(rows)
    rows_p[0:KR, :] = rows_hi
    rows_p[KR : 2 * KR, :] = rows_lo
    masks = [fx * fy, fx * (1.0 - fy), (1.0 - fx) * fy, (1.0 - fx) * (1.0 - fy)]
    for g in range(4):
        m = masks[g].astype(bf16)
        rows_g[g * KR : (g + 1) * KR, :] = rows_hi * m
        rows_g[4 * KR + g * KR : 4 * KR + (g + 1) * KR, :] = rows_lo * m

    for x in range(XL):
        loads[x].wait()
        def cast(i, c, x=x):
            at = pl.ds(i * VB, VB)
            hi, lo = split(draw[x, at, :])
            fhi[at, x * NY : (x + 1) * NY] = hi
            flo[at, x * NY : (x + 1) * NY] = lo
            return c
        lax.fori_loop(0, NB, cast, 0)
    first = dot(rows_p[...], fhi[...])
    moment = first[0:KR] + first[KR : 2 * KR] + dot(rows_p[0:KR, :], flo[...])

    pl.semaphore_wait(barrier, 13)

    axes = ((px, lambda o: device(slab, o, py, pz)), (pz, lambda o: device(slab, px, py, o)))

    def exchange(buf, stage, it, piece):
        me, to = axes[(stage + piece) % 2]
        sent = []
        for d in range(1, 4):
            copy = pltpu.make_async_remote_copy(
                src_ref=buf.at[it, piece, me],
                dst_ref=buf.at[it, piece, me],
                send_sem=bsend.at[it, stage, piece, d - 1],
                recv_sem=brecv.at[it, stage, piece, d - 1],
                device_id=to((me + d) % 4),
                device_id_type=MESH,
            )
            copy.start()
            sent.append(copy)
        return sent

    def arrived(buf, stage, it, piece):
        me, to = axes[(stage + piece) % 2]
        for d in range(1, 4):
            source = (me + 4 - d) % 4
            pltpu.make_async_remote_copy(
                src_ref=buf.at[it, piece, source],
                dst_ref=buf.at[it, piece, source],
                send_sem=bsend.at[it, stage, piece, d - 1],
                recv_sem=brecv.at[it, stage, piece, d - 1],
                device_id=to(source),
                device_id_type=MESH,
            ).wait_recv()
        return (buf[it, piece, 0] + buf[it, piece, 1]) + (buf[it, piece, 2] + buf[it, piece, 3])

    def spread(it, piece):
        sent = []
        for d in range(1, 8):
            copy = pltpu.make_async_remote_copy(
                src_ref=b3.at[it, piece, group],
                dst_ref=b3.at[it, piece, group],
                send_sem=ysend.at[it, piece, d - 1],
                recv_sem=yrecv.at[it, piece, d - 1],
                device_id=yz[d - 1],
                device_id_type=MESH,
            )
            copy.start()
            sent.append(copy)
        return sent

    def spread_arrived(it, piece):
        for d in range(1, 8):
            source = (group + 8 - d) % 8
            pltpu.make_async_remote_copy(
                src_ref=b3.at[it, piece, source],
                dst_ref=b3.at[it, piece, source],
                send_sem=ysend.at[it, piece, d - 1],
                recv_sem=yrecv.at[it, piece, d - 1],
                device_id=yz[d - 1],
                device_id_type=MESH,
            ).wait_recv()

    def start_reduce(it, value):
        sent = []
        for piece in range(2):
            b1[it, piece, axes[piece % 2][0]] = value[:, piece * HALF : (piece + 1) * HALF]
            sent += exchange(b1, 0, it, piece)
        return sent

    def second_stage(it):
        sent = []
        for piece in range(2):
            total = arrived(b1, 0, it, piece)
            b2[it, piece, axes[(1 + piece) % 2][0]] = total
            sent += exchange(b2, 1, it, piece)
        return sent

    def third_stage(it):
        sent = []
        for piece in range(2):
            b3[it, piece, group] = arrived(b2, 1, it, piece)
            sent += spread(it, piece)
        return sent

    sent = start_reduce(0, moment)
    for d in range(1, 4):
        copy = pltpu.make_async_remote_copy(
            src_ref=collision,
            dst_ref=cbuf.at[slab],
            send_sem=csend.at[d - 1],
            recv_sem=crecv.at[d - 1],
            device_id=device((slab + d) % 4, px, py, pz),
            device_id_type=MESH,
        )
        copy.start()
        sent.append(copy)
    cbuf[slab] = collision[...]

    rows_t[...] = jnp.zeros_like(rows_t)
    inflow = wall_values[...] * wall_kind[...].astype(f32)
    rate_x = jnp.abs(cx) * NX
    rate_y = jnp.abs(cy) * NY
    rows_t[0:1, :] = rate_x
    rows_t[1:2, :] = rate_y / (1.0 + rate_y)
    rows_t[2:3, :] = 1.0 / (1.0 + rate_y)
    rows_t[3:4, :] = jnp.where(low_side, inflow[0:1], inflow[1:2])
    rows_t[4:5, :] = fx
    rows_t[5:6, :] = fy
    for i in range(NB):
        at = slice(i * VB, (i + 1) * VB)
        col[at, :] = jnp.transpose(rows_t[:, at])
    factor = 4.0 / 45.0 * heat
    psi = jnp.concatenate(
        [one, 2.0 * cx, 2.0 * cy, 2.0 * cz, square - 1.5, factor * cx, factor * cy, factor * cz],
        axis=0,
    )
    psi_hi = psi.astype(bf16).astype(f32)
    psi_lo = psi - psi_hi
    for g in range(4):
        rows_t[g * 32 : g * 32 + 8, :] = psi_hi * masks[g]
        rows_t[g * 32 + 8 : g * 32 + 16, :] = psi_hi * masks[g]
        rows_t[g * 32 + 16 : g * 32 + 24, :] = psi_lo * masks[g]
        rows_t[g * 32 + 24 : g * 32 + 32, :] = psi_lo * masks[g]
    for i in range(NB):
        at = slice(i * VB, (i + 1) * VB)
        shp[at, :] = jnp.transpose(rows_t[:, at]).astype(bf16)

    lane = lanes((VB, NY))

    def send_out(buf, target, send, recv, it, i, to):
        at = pl.ds(i * VB, VB)
        pltpu.make_async_remote_copy(
            src_ref=buf.at[it, at],
            dst_ref=target.at[it, at],
            send_sem=send.at[it, i],
            recv_sem=recv.at[it, i],
            device_id=device(to, px, py, pz),
            device_id_type=MESH,
        ).start()

    def wait_in(target, send, recv, it, i):
        at = pl.ds(i * VB, VB)
        pltpu.make_async_remote_copy(
            src_ref=target.at[it, at],
            dst_ref=target.at[it, at],
            send_sem=send.at[it, i],
            recv_sem=recv.at[it, i],
            device_id=device(partner, px, py, pz),
            device_id_type=MESH,
        ).wait_recv()

    def wait_out(buf, target, send, recv, it, i):
        at = pl.ds(i * VB, VB)
        pltpu.make_async_remote_copy(
            src_ref=buf.at[it, at],
            dst_ref=target.at[it, at],
            send_sem=send.at[it, i],
            recv_sem=recv.at[it, i],
            device_id=device(partner, px, py, pz),
            device_id_type=MESH,
        ).wait_send()

    own = collision[...]
    own_back = mirrored(jnp.concatenate([own, own], axis=0))

    def sweep_source(fields, at, it, i):
        total = inv_own[0, at, :] * fields[0]
        gd[0, at, :] = total
        for q in range(1, XL):
            total = fac[PAD + q, at, :] * total + inv_own[q, at, :] * fields[q]
            gd[q, at, :] = total

        @pl.when(edge)
        def _():
            outa[it, at, :] = prod[at, :] * near[it, at, :] + total
            send_out(outa, near, nsend, nrecv, it, i, partner)

    def prepare(i, c):
        at = pl.ds(i * VB, VB)
        cols = col[at, :]
        wide = lambda k: jnp.broadcast_to(cols[:, k : k + 1], (VB, NY))
        a = wide(0)
        ascale[at, :] = a
        power = wide(1)
        for k, step in enumerate(STEPS):
            ycoef[k, at, :] = jnp.where(lane >= step, power, 0.0)
            power = power * power
        bscale[at, :] = wide(2)
        fxv, fyv = wide(4), wide(5)
        fxs[at, :] = fxv
        fys[at, :] = fyv
        forward, upward = fxv > 0.5, fyv > 0.5

        @pl.when(edge)
        def _():
            for it in range(ITERS):
                near[it, at, :] = wide(3)

        index = jnp.where(upward, lane, NY - 1 - lane)
        product = None
        fields = []
        for q in range(XL):
            m = XL - 1 - q
            rate = jnp.where(
                forward,
                jnp.where(upward, own[q : q + 1], own_back[q : q + 1]),
                jnp.where(upward, own[m : m + 1], own_back[m : m + 1]),
            )
            inv = 1.0 / (1.0 + a + rate)
            f = a * inv
            inv_own[q, at, :] = inv
            fac[PAD + q, at, :] = f
            wgt[PAD + q, at, :] = rate * inv
            product = f if product is None else product * f
            picked = jnp.where(forward, draw[q, at, :], draw[m, at, :])
            fields.append(jnp.take_along_axis(picked, index, axis=1))
        prod[at, :] = product
        sweep_source(fields, at, 0, i)
        return c

    lax.fori_loop(0, NB, prepare, 0)

    def chain_across(it):
        @pl.when(middle)
        def _():
            def step(i, c):
                at = pl.ds(i * VB, VB)
                wait_in(near, nsend, nrecv, it, i)
                outa[it, at, :] = prod[at, :] * near[it, at, :] + gd[XL - 1, at, :]
                send_out(outa, far, fsend, frecv, it, i, across)
                return c
            lax.fori_loop(0, NB, step, 0)

    def chain_back(it):
        @pl.when(middle)
        def _():
            def step(i, c):
                at = pl.ds(i * VB, VB)
                wait_in(far, fsend, frecv, it, i)
                outb[it, at, :] = prod[at, :] * far[it, at, :] + gd[XL - 1, at, :]
                pltpu.make_async_remote_copy(
                    src_ref=outb.at[it, at],
                    dst_ref=far.at[it, at],
                    send_sem=nsend.at[it, i],
                    recv_sem=frecv.at[it, i],
                    device_id=device(partner, px, py, pz),
                    device_id_type=MESH,
                ).start()
                return c
            lax.fori_loop(0, NB, step, 0)

    def drain_chain(it):
        @pl.when(middle)
        def _():
            def step(i, c):
                wait_out(outa, far, fsend, frecv, it, i)
                wait_out(outb, far, nsend, frecv, it, i)
                return c
            lax.fori_loop(0, NB, step, 0)

        @pl.when(edge)
        def _():
            def step(i, c):
                wait_out(outa, near, nsend, nrecv, it, i)
                return c
            lax.fori_loop(0, NB, step, 0)

    sent += second_stage(0)
    chain_across(0)

    for d in range(1, 4):
        source = (slab + 4 - d) % 4
        pltpu.make_async_remote_copy(
            src_ref=collision,
            dst_ref=cbuf.at[source],
            send_sem=csend.at[d - 1],
            recv_sem=crecv.at[d - 1],
            device_id=device(source, px, py, pz),
            device_id_type=MESH,
        ).wait_recv()
    crow[...] = jnp.zeros_like(crow)
    everywhere = jnp.concatenate([cbuf[s] for s in range(SLABS)], axis=0)
    turned = mirrored(everywhere)
    for i in range(NX):
        crow[0, PAD + i] = jnp.broadcast_to(everywhere[i : i + 1], (8, NY))
        crow[1, PAD + i] = jnp.broadcast_to(turned[i : i + 1], (8, NY))

    def upstream(start, stop):
        def at_cell(r, c):
            ahead = XL * slab + r
            behind = XL * slab + PAD + NX - 1 - r
            c_ff = crow[0, ahead][0:1]
            c_fb = crow[1, ahead][0:1]
            c_bf = crow[0, behind][0:1]
            c_bb = crow[1, behind][0:1]
            def block(i, c):
                at = pl.ds(i * VB, VB)
                a = ascale[at, :]
                forward, upward = fxs[at, :] > 0.5, fys[at, :] > 0.5
                rate = jnp.where(
                    forward, jnp.where(upward, c_ff, c_fb), jnp.where(upward, c_bf, c_bb)
                )
                inv = 1.0 / (1.0 + a + rate)
                fac[r, at, :] = a * inv
                wgt[r, at, :] = rate * inv
                return c
            lax.fori_loop(0, NB, block, 0)
            return c
        lax.fori_loop(start, stop, at_cell, 0)

    upstream(0, 5)
    sent += third_stage(0)
    upstream(5, PAD)
    chain_back(0)

    cell = lanes((8, NY))
    sub = lax.broadcasted_iota(jnp.int32, (8, NY), 0)

    def above(value):
        return jnp.where(cell < NY - 1, pltpu.roll(value, NY - 1, 1), 0.0)

    def below(value):
        return jnp.where(cell >= 1, pltpu.roll(value, 1, 1), 0.0)

    def macro(it):
        for piece in range(2):
            spread_arrived(it, piece)
        head, flux = [], []
        for i in range(NX):
            s, x = i // XL, i % XL
            piece, at = x // 2, slice((x % 2) * NY, (x % 2 + 1) * NY)
            head.append(b3[it, piece, s, 0:8, at] + b3[it, piece, 4 + s, 0:8, at])
            flux.append(b3[it, piece, s, 8:16, at] + b3[it, piece, 4 + s, 8:16, at])
        nothing = jnp.zeros((8, NY), f32)
        target, kappa, down = [], [], []
        for i in range(NX):
            a, b = head[i], flux[i]
            cross = jnp.concatenate([a[2:3], b[2:3], b[5:6], b[6:7], a[6:7], b[7:8], b[7:8], b[7:8]], axis=0)
            right = flux[i + 1] if i + 1 < NX else nothing
            left = flux[i - 1] if i > 0 else nothing
            target.append(a - (0.5 * (right - left) + 0.5 * (above(cross) - below(cross))))
            stiff = 1.0 / crow[0, PAD + i]
            kappa.append(stiff)
            down.append(1.0 / (1.0 + 4.0 * stiff))
        settled = head
        for _ in range(JACOBI):
            after = []
            for i in range(NX):
                right = settled[i + 1] if i + 1 < NX else nothing
                left = settled[i - 1] if i > 0 else nothing
                around = right + left + above(settled[i]) + below(settled[i])
                after.append((target[i] + kappa[i] * around) * down[i])
            settled = after
        dpad[...] = jnp.zeros_like(dpad)
        for i in range(NX):
            drive = jnp.where(sub < 5, settled[i], head[i])
            drive_s[i] = drive
            hi, lo = split(drive)
            dpad[0, PAD + i] = jnp.concatenate([hi, lo], axis=0)
            hi, lo = split(mirrored(drive))
            dpad[1, PAD + i] = jnp.concatenate([hi, lo], axis=0)
        for r in range(NX):
            ahead = XL * slab + r
            behind = XL * slab + PAD + NX - 1 - r
            at = slice(r * NY, (r + 1) * NY)
            for g, tile in enumerate(
                (dpad[0, ahead], dpad[1, ahead], dpad[0, behind], dpad[1, behind])
            ):
                rhs[g * 32 : g * 32 + 16, at] = tile
                rhs[g * 32 + 16 : g * 32 + 32, at] = tile

    def main(it):
        last = it == ITERS - 1

        def block(i, c):
            at = pl.ds(i * VB, VB)
            eq = dot(shp[at, :], rhs[...])
            enter = wgt[0, at, :] * eq[:, 0:NY]
            for r in range(1, PAD):
                enter = fac[r, at, :] * enter + wgt[r, at, :] * eq[:, r * NY : (r + 1) * NY]

            @pl.when(edge)
            def _():
                wait_in(far, fsend, frecv, it, i)

            forward = fxs[at, :] > 0.5
            from_near = jnp.where(low_side, fxs[at, :], 1.0 - fxs[at, :]) > 0.5
            enter = enter + jnp.where(from_near, near[it, at, :], far[it, at, :])
            fields = []
            for q in range(XL):
                r = PAD + q
                enter = fac[r, at, :] * enter + wgt[r, at, :] * eq[:, r * NY : (r + 1) * NY]
                h = (gd[q, at, :] + enter) * bscale[at, :]
                for k, step in enumerate(STEPS):
                    h = h + ycoef[k, at, :] * pltpu.roll(h, step, 1)
                if last:
                    gd[q, at, :] = h
                else:
                    hi, lo = split(h)
                    fhi[at, q * NY : (q + 1) * NY] = hi
                    flo[at, q * NY : (q + 1) * NY] = lo
                    fields.append(h)
            if last:
                for q in range(XL):
                    pltpu.make_async_copy(gd.at[q, at], out.at[q, at], osem.at[q, i]).start()
            else:
                sweep_source(fields, at, it + 1, i)
            return c

        lax.fori_loop(0, NB, block, 0)

    for it in range(ITERS):
        macro(it)
        main(it)
        if it < ITERS - 1:
            first = dot(rows_g[...], fhi[...])
            groups = first[0 : 4 * KR] + first[4 * KR : 8 * KR] + dot(rows_g[0 : 4 * KR, :], flo[...])
            turn = lambda t: jnp.concatenate(
                [t[:, x * NY : (x + 1) * NY] for x in reversed(range(XL))], axis=1
            )
            up = groups[0:KR] + turn(groups[2 * KR : 3 * KR])
            down = groups[KR : 2 * KR] + turn(groups[3 * KR : 4 * KR])
            moment = up + jnp.concatenate(
                [mirrored(down[:, x * NY : (x + 1) * NY]) for x in range(XL)], axis=1
            )
            sent += start_reduce(it + 1, moment)
            chain_across(it + 1)
            sent += second_stage(it + 1)
            chain_back(it + 1)
            sent += third_stage(it + 1)

    for x in range(XL):
        settled_out[:, x, :] = drive_s[XL * slab + x][0:5]

    def drain(i, c):
        at = pl.ds(i * VB, VB)
        for q in range(XL):
            pltpu.make_async_copy(gd.at[q, at], out.at[q, at], osem.at[q, i]).wait()
        return c

    lax.fori_loop(0, NB, drain, 0)
    for it in range(ITERS):
        drain_chain(it)
    for copy in sent:
        copy.wait_send()


def order_kernel(field, speeds, settled, out, settled_out):
    signs = jnp.transpose(speeds[...])
    forward = jnp.broadcast_to(signs[:, 0:1], (VB, NY)) >= 0
    upward = jnp.broadcast_to(signs[:, 1:2], (VB, NY)) >= 0
    lane = lanes((VB, NY))
    index = jnp.where(upward, lane, NY - 1 - lane)
    for x in range(XL):
        picked = jnp.where(forward, field[x], field[XL - 1 - x])
        out[pl.ds(x, VB, stride=XL), :] = jnp.take_along_axis(picked, index, axis=1)
    settled_out[...] = settled[...]


def on_device(dist, speeds, weights, collision, wall_values, wall_kind):
    vmem = pl.BlockSpec(memory_space=pltpu.VMEM)
    hbm = pl.BlockSpec(memory_space=pl.ANY)
    dma = pltpu.SemaphoreType.DMA
    full = (V, NY)
    scratch = [
        pltpu.VMEM((XL, *full), f32),
        pltpu.VMEM((XL, *full), f32),
        pltpu.VMEM((V, XL * NY), bf16),
        pltpu.VMEM((V, XL * NY), bf16),
        pltpu.VMEM((NX, *full), f32),
        pltpu.VMEM((NX, *full), f32),
        pltpu.VMEM((XL, *full), f32),
        pltpu.VMEM(full, f32),
        pltpu.VMEM((len(STEPS), *full), f32),
        pltpu.VMEM(full, f32),
        pltpu.VMEM(full, f32),
        pltpu.VMEM(full, f32),
        pltpu.VMEM(full, f32),
        pltpu.VMEM((ITERS, *full), f32),
        pltpu.VMEM((ITERS, *full), f32),
        pltpu.VMEM((ITERS, *full), f32),
        pltpu.VMEM((ITERS, *full), f32),
        pltpu.VMEM((128, V), f32),
        pltpu.VMEM((2 * KR, V), bf16),
        pltpu.VMEM((8 * KR, V), bf16),
        pltpu.VMEM((V, 128), bf16),
        pltpu.VMEM((V, 128), f32),
        pltpu.VMEM((ITERS, 2, 4, KR, HALF), f32),
        pltpu.VMEM((ITERS, 2, 4, KR, HALF), f32),
        pltpu.VMEM((ITERS, 2, 8, KR, HALF), f32),
        pltpu.VMEM((SLABS, XL, NY), f32),
        pltpu.VMEM((2, NX + 2 * PAD, 8, NY), f32),
        pltpu.VMEM((2, NX + 2 * PAD, 16, NY), bf16),
        pltpu.VMEM((128, NX * NY), bf16),
        pltpu.VMEM((NX, 8, NY), f32),
        dma((XL,)),
        dma((XL, NB)),
        dma((ITERS, 2, 2, 3)),
        dma((ITERS, 2, 2, 3)),
        dma((ITERS, 2, 7)),
        dma((ITERS, 2, 7)),
        dma((3,)),
        dma((3,)),
        dma((ITERS, NB)),
        dma((ITERS, NB)),
        dma((ITERS, NB)),
        dma((ITERS, NB)),
    ]
    field, settled = pl.pallas_call(
        transport_kernel,
        out_shape=(
            jax.ShapeDtypeStruct((XL, *full), f32),
            jax.ShapeDtypeStruct((5, XL, NY), f32),
        ),
        in_specs=[hbm] + [vmem] * 5,
        out_specs=(hbm, vmem),
        scratch_shapes=scratch,
        compiler_params=pltpu.CompilerParams(
            collective_id=0, has_side_effects=True, vmem_limit_bytes=60 * 1024 * 1024
        ),
        name="transport",
    )(dist, speeds, weights[None], collision, wall_values, wall_kind)
    rows, settled = pl.pallas_call(
        order_kernel,
        grid=(NB,),
        out_shape=(
            jax.ShapeDtypeStruct((V * XL, NY), f32),
            jax.ShapeDtypeStruct((5, XL, NY), f32),
        ),
        in_specs=[
            pl.BlockSpec((XL, VB, NY), lambda i: (0, i, 0)),
            pl.BlockSpec((3, VB), lambda i: (0, i)),
            pl.BlockSpec((5, XL, NY), lambda i: (0, 0, 0)),
        ],
        out_specs=(
            pl.BlockSpec((VB * XL, NY), lambda i: (i, 0)),
            pl.BlockSpec((5, XL, NY), lambda i: (0, 0, 0)),
        ),
        name="order",
    )(field, speeds, settled)
    return rows.reshape(V, XL, NY), settled


def solution(mesh):
    return jax.shard_map(
        on_device,
        mesh=mesh,
        in_specs=(
            P("vel", "slab", None),
            P(None, "vel"),
            P("vel"),
            P("slab", None),
            P(None, "vel"),
            P(None, "vel"),
        ),
        out_specs=(P("vel", "slab", None), P(None, "slab", None)),
        check_vma=False,
    )
```

time: 339 us -> 58.6 us (0.17); the launches traced: 335 us -> 58.3 us
  local copies, waits for them, and re-layouts: 140 us -> 1.27 us
  other arithmetic: 71.5 us -> 0 us
  Pallas kernels: 0 us -> 56.4 us
  starting transfers between devices: 45.4 us -> 0 us
  waiting for transfers between devices: 45.4 us -> 0 us
  blocking collectives: 22.7 us -> 0 us
  matrix products: 7.11 us -> 0 us
    pallas_call x0 -> x2, Pallas kernels: none -> 56.4 us  [the longest x1 50.9 us: on_device(): pl.pallas_call(transport_kernel, out_shape=(jax.ShapeDtypeStruct((XL, *fu...]
    slice x53 -> x0, local copies, waits for them, and re-layouts: 54.3 us -> none  [the longest x46 53.6 us: sweep_across(): return lax.associative_scan(combine, (factor, source), axis=axis)]
    add x46 -> x0, other arithmetic: 41.1 us -> none  [the longest x25 21.6 us: combine(): return (earlier[0] * later[0], later[0] * earlier[1] + later[1])]
    all_to_all x3 -> x0, waiting for transfers between devices: 38.6 us -> none  [from_everyone(): lax.all_to_all(jnp.broadcast_to(shard[None], (devices, *shard.shape)), ax...]
    rev x4 -> x0, local copies, waits for them, and re-layouts: 36 us -> none  [the longest x2 20.5 us: along_y(): source = jnp.where(forward, source, source[:, :, ::-1])]
    pad x30 -> x0, local copies, waits for them, and re-layouts: 29.6 us -> none  [sweep_across(): return lax.associative_scan(combine, (factor, source), axis=axis)]
    ppermute x8 -> x0, starting transfers between devices: 25.2 us -> none  [the longest x4 17.5 us: extended_2(): lax.ppermute(tail, axis, [(i, (i + 1) % count) for i in range(ends)])]
    all_to_all x3 -> x0, starting transfers between devices: 20.2 us -> none  [from_everyone(): lax.all_to_all(jnp.broadcast_to(shard[None], (devices, *shard.shape)), ax...]
  transfers between devices with their start and end apart: 11 -> 0, of which waited for: 6 -> 0; matrix products, arithmetic and copies ran while one was open for 4% -> 0% of each run, Pallas kernels for 0% -> 0%
where the time goes in v1:
time: 58.6 us; the launch traced here: 58.3 us
  Pallas kernels  56.4 us (96%)
  local copies, waits for them, and re-layouts  1.27 us (2%)
  between operations  0.64 us (1%)
    pallas_call x1, Pallas kernels, on_device(): pl.pallas_call(transport_kernel, out_shape=(jax.ShapeDtypeStruct((XL, *fu...  50.9 us
    pallas_call x1, Pallas kernels, on_device(): pl.pallas_call(order_kernel, grid=(NB,), out_shape=(jax.ShapeDtypeStruct(...  5.45 us
    broadcast_in_dim x1, local copies, waits for them, and re-layouts, on_device(): weights[None]  1.27 us

profile of v1, /device:TPU:1, one launch (start us, length us, event | category | flops | bytes accessed | tf_op | source)
XLA Modules:
  0.0 58.3 jit_solution(3100471504019387957)
XLA Ops:
  0.6 1.3 %broadcast_in_dim.3.weights = f32[1,768]{1,0:T(1,128)} reshape(f32[768]{0:T(1024)} %param.8) | data formatting | bytes 6144 | tf_op jit(solution)/shard_map/broadcast_in_dim | solution.py:643
  1.9 50.9 %transport.1 = (f32[4,768,128]{2,1,0:T(8,128)}, f32[5,4,128]{2,1,0:T(4,128)}) custom-call(f32[768,4,128]{2,1,0:T(4,128)} %dist.1, f32[3,768]{1,0:T(4,128)} %speeds.3, f32[1,768]{1,0:T(1,128)} %broadcast_in_dim.3.weights, f32[4,128]{1,0:T(4,128)} %collision.1, f32[2,768]{1,0:T(2,128)} %wall_values.1, s32[2,768]{1,0:T(2,128)} %wall_kind.1), custom_call_target="tpu_custom_call" | custom-call | tf_op jit(solution)/shard_map/transport/pallas_call | solution.py:630
  52.8 5.5 %order.1 = (f32[3072,128]{1,0:T(8,128)}, f32[5,4,128]{2,1,0:T(4,128)}) custom-call(f32[4,768,128]{2,1,0:T(8,128)} %get-tuple-element.6.field, f32[3,768]{1,0:T(4,128)} %speeds.3, f32[5,4,128]{2,1,0:T(4,128)} %get-tuple-element.7.settled), custom_call_target="tpu_custom_call" | custom-call | tf_op jit(solution)/shard_map/order/pallas_call | solution.py:644

commit v2 on v1

--- a/solution.py
+++ b/solution.py
@@ -17,6 +17,8 @@
 NB = V // VB
 PAD = NX - XL
 KR = 16
+ROWS = 13
+LAG = 2
 HALF = XL * NY // 2
 STEPS = (1, 2, 4, 8, 16, 32, 64)
 
@@ -43,12 +45,13 @@
 
 
 def transport_kernel(
-    dist, speeds, weights, collision, wall_values, wall_kind,
+    dist, speeds_in, weights_in, collision_in, values_in, kind_in,
     out, settled_out,
     draw, gd, fhi, flo, fac, wgt, inv_own, prod, ycoef, ascale, bscale, fxs, fys,
     near, far, outa, outb, rows_t, rows_p, rows_g, shp, col,
     b1, b2, b3, cbuf, crow, dpad, rhs, drive_s,
-    dsem, osem, bsend, brecv, ysend, yrecv, csend, crecv, nsend, nrecv, fsend, frecv,
+    speeds, weights, collision, wall_values, wall_kind,
+    dsem, ssem, bsend, brecv, ysend, yrecv, csend, crecv, nsend, nrecv, fsend, frecv,
 ):
     slab = lax.axis_index("slab")
     vel = lax.axis_index("vel")
@@ -67,7 +70,14 @@
     loads = [
         pltpu.make_async_copy(dist.at[:, x, :], draw.at[x], dsem.at[x]) for x in range(XL)
     ]
-    for load in loads:
+    small = [
+        pltpu.make_async_copy(source, target, ssem.at[n])
+        for n, (source, target) in enumerate((
+            (speeds_in, speeds), (weights_in, weights), (collision_in, collision),
+            (values_in, wall_values), (kind_in, wall_kind),
+        ))
+    ]
+    for load in small + loads:
         load.start()
 
     peers = []
@@ -84,8 +94,10 @@
     for peer in peers + yz:
         pl.semaphore_signal(barrier, inc=1, device_id=peer, device_id_type=MESH)
 
+    for load in small:
+        load.wait()
     cx, cy, cz = speeds[0:1, :], speeds[1:2, :], speeds[2:3, :]
-    wt = weights[0:1, :]
+    wt = weights[...].reshape(1, V)
     square = cx * cx + cy * cy + cz * cz
     third = square / 3.0
     heat = square - 2.5
@@ -93,7 +105,7 @@
     zero = jnp.zeros_like(cx)
     phi = [
         one, cx, cy, cz, 2.0 / 3.0 * square - 1.0, cx * heat, cy * heat, cz * heat,
-        cx, cx * cx - third, cx * cy, cx * cz, cx * heat, cy * cy - third, cy * cz, zero,
+        cx * cx - third, cx * cy, cx * cz, cy * cy - third, cy * cz, zero, zero, zero,
     ]
     scale = wt / VELS
     fx = jnp.where(cx >= 0, 1.0, 0.0)
@@ -184,7 +196,7 @@
     def start_reduce(it, value):
         sent = []
         for piece in range(2):
-            b1[it, piece, axes[piece % 2][0]] = value[:, piece * HALF : (piece + 1) * HALF]
+            b1[it, piece, axes[piece % 2][0]] = value[0:ROWS, piece * HALF : (piece + 1) * HALF]
             sent += exchange(b1, 0, it, piece)
         return sent
 
@@ -284,6 +296,12 @@
     own = collision[...]
     own_back = mirrored(jnp.concatenate([own, own], axis=0))
 
+    def pass_on(it, i):
+        at = pl.ds(i * VB, VB)
+        wait_in(near, nsend, nrecv, it, i)
+        outa[it, at, :] = prod[at, :] * near[it, at, :] + gd[XL - 1, at, :]
+        send_out(outa, far, fsend, frecv, it, i, across)
+
     def sweep_source(fields, at, it, i):
         total = inv_own[0, at, :] * fields[0]
         gd[0, at, :] = total
@@ -295,6 +313,10 @@
         def _():
             outa[it, at, :] = prod[at, :] * near[it, at, :] + total
             send_out(outa, near, nsend, nrecv, it, i, partner)
+
+        @pl.when(jnp.logical_and(middle, i >= LAG))
+        def _():
+            pass_on(it, i - LAG)
 
     def prepare(i, c):
         at = pl.ds(i * VB, VB)
@@ -345,12 +367,9 @@
         @pl.when(middle)
         def _():
             def step(i, c):
-                at = pl.ds(i * VB, VB)
-                wait_in(near, nsend, nrecv, it, i)
-                outa[it, at, :] = prod[at, :] * near[it, at, :] + gd[XL - 1, at, :]
-                send_out(outa, far, fsend, frecv, it, i, across)
+                pass_on(it, i)
                 return c
-            lax.fori_loop(0, NB, step, 0)
+            lax.fori_loop(NB - LAG, NB, step, 0)
 
     def chain_back(it):
         @pl.when(middle)
@@ -431,8 +450,8 @@
 
     upstream(0, 5)
     sent += third_stage(0)
+    chain_back(0)
     upstream(5, PAD)
-    chain_back(0)
 
     cell = lanes((8, NY))
     sub = lax.broadcasted_iota(jnp.int32, (8, NY), 0)
@@ -451,14 +470,17 @@
             s, x = i // XL, i % XL
             piece, at = x // 2, slice((x % 2) * NY, (x % 2 + 1) * NY)
             head.append(b3[it, piece, s, 0:8, at] + b3[it, piece, 4 + s, 0:8, at])
-            flux.append(b3[it, piece, s, 8:16, at] + b3[it, piece, 4 + s, 8:16, at])
+            flux.append(b3[it, piece, s, 8:ROWS, at] + b3[it, piece, 4 + s, 8:ROWS, at])
         nothing = jnp.zeros((8, NY), f32)
+        along = [
+            jnp.concatenate([a[1:2], b[0:3], a[5:6], a[5:8]], axis=0) for a, b in zip(head, flux)
+        ]
         target, kappa, down = [], [], []
         for i in range(NX):
             a, b = head[i], flux[i]
-            cross = jnp.concatenate([a[2:3], b[2:3], b[5:6], b[6:7], a[6:7], b[7:8], b[7:8], b[7:8]], axis=0)
-            right = flux[i + 1] if i + 1 < NX else nothing
-            left = flux[i - 1] if i > 0 else nothing
+            cross = jnp.concatenate([a[2:3], b[1:2], b[3:5], a[6:7], a[5:8]], axis=0)
+            right = along[i + 1] if i + 1 < NX else nothing
+            left = along[i - 1] if i > 0 else nothing
             target.append(a - (0.5 * (right - left) + 0.5 * (above(cross) - below(cross))))
             stiff = 1.0 / crow[0, PAD + i]
             kappa.append(stiff)
@@ -514,16 +536,18 @@
                 h = (gd[q, at, :] + enter) * bscale[at, :]
                 for k, step in enumerate(STEPS):
                     h = h + ycoef[k, at, :] * pltpu.roll(h, step, 1)
-                if last:
-                    gd[q, at, :] = h
-                else:
+                fields.append(h)
+                if not last:
                     hi, lo = split(h)
                     fhi[at, q * NY : (q + 1) * NY] = hi
                     flo[at, q * NY : (q + 1) * NY] = lo
-                    fields.append(h)
             if last:
-                for q in range(XL):
-                    pltpu.make_async_copy(gd.at[q, at], out.at[q, at], osem.at[q, i]).start()
+                index = jnp.where(fys[at, :] > 0.5, lane, NY - 1 - lane)
+                for x in range(XL):
+                    picked = jnp.where(forward, fields[x], fields[XL - 1 - x])
+                    out[pl.ds(i * VB * XL + x, VB, stride=XL), :] = jnp.take_along_axis(
+                        picked, index, axis=1
+                    )
             else:
                 sweep_source(fields, at, it + 1, i)
             return c
@@ -553,34 +577,15 @@
     for x in range(XL):
         settled_out[:, x, :] = drive_s[XL * slab + x][0:5]
 
-    def drain(i, c):
-        at = pl.ds(i * VB, VB)
-        for q in range(XL):
-            pltpu.make_async_copy(gd.at[q, at], out.at[q, at], osem.at[q, i]).wait()
-        return c
-
-    lax.fori_loop(0, NB, drain, 0)
     for it in range(ITERS):
         drain_chain(it)
     for copy in sent:
         copy.wait_send()
 
 
-def order_kernel(field, speeds, settled, out, settled_out):
-    signs = jnp.transpose(speeds[...])
-    forward = jnp.broadcast_to(signs[:, 0:1], (VB, NY)) >= 0
-    upward = jnp.broadcast_to(signs[:, 1:2], (VB, NY)) >= 0
-    lane = lanes((VB, NY))
-    index = jnp.where(upward, lane, NY - 1 - lane)
-    for x in range(XL):
-        picked = jnp.where(forward, field[x], field[XL - 1 - x])
-        out[pl.ds(x, VB, stride=XL), :] = jnp.take_along_axis(picked, index, axis=1)
-    settled_out[...] = settled[...]
-
-
 def on_device(dist, speeds, weights, collision, wall_values, wall_kind):
     vmem = pl.BlockSpec(memory_space=pltpu.VMEM)
-    hbm = pl.BlockSpec(memory_space=pl.ANY)
+    hbm = pl.BlockSpec(memory_space=pltpu.HBM)
     dma = pltpu.SemaphoreType.DMA
     full = (V, NY)
     scratch = [
@@ -606,16 +611,21 @@
         pltpu.VMEM((8 * KR, V), bf16),
         pltpu.VMEM((V, 128), bf16),
         pltpu.VMEM((V, 128), f32),
-        pltpu.VMEM((ITERS, 2, 4, KR, HALF), f32),
-        pltpu.VMEM((ITERS, 2, 4, KR, HALF), f32),
-        pltpu.VMEM((ITERS, 2, 8, KR, HALF), f32),
+        pltpu.VMEM((ITERS, 2, 4, ROWS, HALF), f32),
+        pltpu.VMEM((ITERS, 2, 4, ROWS, HALF), f32),
+        pltpu.VMEM((ITERS, 2, 8, ROWS, HALF), f32),
         pltpu.VMEM((SLABS, XL, NY), f32),
         pltpu.VMEM((2, NX + 2 * PAD, 8, NY), f32),
         pltpu.VMEM((2, NX + 2 * PAD, 16, NY), bf16),
         pltpu.VMEM((128, NX * NY), bf16),
         pltpu.VMEM((NX, 8, NY), f32),
+        pltpu.VMEM((3, V), f32),
+        pltpu.VMEM((V,), f32),
+        pltpu.VMEM((XL, NY), f32),
+        pltpu.VMEM((2, V), f32),
+        pltpu.VMEM((2, V), jnp.int32),
         dma((XL,)),
-        dma((XL, NB)),
+        dma((5,)),
         dma((ITERS, 2, 2, 3)),
         dma((ITERS, 2, 2, 3)),
         dma((ITERS, 2, 7)),
@@ -627,38 +637,23 @@
         dma((ITERS, NB)),
         dma((ITERS, NB)),
     ]
-    field, settled = pl.pallas_call(
+    rows, settled = pl.pallas_call(
         transport_kernel,
-        out_shape=(
-            jax.ShapeDtypeStruct((XL, *full), f32),
-            jax.ShapeDtypeStruct((5, XL, NY), f32),
-        ),
-        in_specs=[hbm] + [vmem] * 5,
-        out_specs=(hbm, vmem),
-        scratch_shapes=scratch,
-        compiler_params=pltpu.CompilerParams(
-            collective_id=0, has_side_effects=True, vmem_limit_bytes=60 * 1024 * 1024
-        ),
-        name="transport",
-    )(dist, speeds, weights[None], collision, wall_values, wall_kind)
-    rows, settled = pl.pallas_call(
-        order_kernel,
-        grid=(NB,),
         out_shape=(
             jax.ShapeDtypeStruct((V * XL, NY), f32),
             jax.ShapeDtypeStruct((5, XL, NY), f32),
         ),
-        in_specs=[
-            pl.BlockSpec((XL, VB, NY), lambda i: (0, i, 0)),
-            pl.BlockSpec((3, VB), lambda i: (0, i)),
-            pl.BlockSpec((5, XL, NY), lambda i: (0, 0, 0)),
-        ],
-        out_specs=(
-            pl.BlockSpec((VB * XL, NY), lambda i: (i, 0)),
-            pl.BlockSpec((5, XL, NY), lambda i: (0, 0, 0)),
+        in_specs=[hbm] * 6,
+        out_specs=(vmem, vmem),
+        scratch_shapes=scratch,
+        compiler_params=pltpu.CompilerParams(
+            collective_id=0, has_side_effects=True, vmem_limit_bytes=50000000
         ),
-        name="order",
-    )(field, speeds, settled)
+        name="transport",
+    )(*(
+        pltpu.with_memory_space_constraint(value, pltpu.HBM)
+        for value in (dist, speeds, weights, collision, wall_values, wall_kind)
+    ))
     return rows.reshape(V, XL, NY), settled
 
 

time: 58.6 us -> 51.5 us (0.88)
  Pallas kernels: 56.4 us -> 49 us
    pallas_call x2 -> x1, Pallas kernels: 56.4 us -> 49 us  [on_device(): pl.pallas_call(transport_kernel, out_shape=(jax.ShapeDtypeStruct((V * XL,...]
    unnamed x0 -> x2, local copies, waits for them, and re-layouts: none -> 1.74 us
    broadcast_in_dim x1 -> x0, local copies, waits for them, and re-layouts: 1.27 us -> none  [on_device(): weights[None]]
where the time goes in v2:
time: 51.5 us; the launch traced here: 51.4 us
  Pallas kernels  49 us (95%)
  local copies, waits for them, and re-layouts  1.74 us (3%)
  between operations  0.64 us (1%)
    pallas_call x1, Pallas kernels, on_device(): pl.pallas_call(transport_kernel, out_shape=(jax.ShapeDtypeStruct((V * XL,...  49 us
    unnamed x2, local copies, waits for them, and re-layouts  1.74 us

profile of v2, /device:TPU:1, one launch (start us, length us, event | category | flops | bytes accessed | tf_op | source)
XLA Modules:
  0.0 51.4 jit_solution(7471987807356000237)
XLA Ops:
  0.6 49.0 %transport.1 = (f32[3072,128]{1,0:T(8,128)S(1)}, f32[5,4,128]{2,1,0:T(4,128)S(1)}) custom-call(f32[768,4,128]{2,1,0:T(4,128)} %dist.1, f32[3,768]{1,0:T(4,128)} %speeds_in.1, f32[768]{0:T(1024)} %weights_in.1, f32[4,128]{1,0:T(4,128)} %collision_in.1, f32[2,768]{1,0:T(2,128)} %values_in.1, s32[2,768]{1,0:T(2,128)} %kind_in.1), custom_call_target="tpu_custom_call" | custom-call | tf_op jit(solution)/shard_map/transport/pallas_call | solution.py:640
  49.6 1.1 %copy.10 = f32[768,4,128]{2,1,0:T(4,128)} copy(f32[768,4,128]{2,1,0:T(4,128)S(1)} %bitcast.1) | data formatting | bytes 3145728
  50.8 0.6 %copy.11 = f32[5,4,128]{2,1,0:T(4,128)} copy(f32[5,4,128]{2,1,0:T(4,128)S(1)} %get-tuple-element.9) | data formatting | bytes 20480

commit v3 on v2

--- a/solution.py
+++ b/solution.py
@@ -15,12 +15,15 @@
 V = VELS // 32
 VB = 128
 NB = V // VB
+CB = 256
+NC = V // CB
 PAD = NX - XL
 KR = 16
 ROWS = 13
-LAG = 2
+LAG = 1
 HALF = XL * NY // 2
-STEPS = (1, 2, 4, 8, 16, 32, 64)
+SEG = NY // 8
+TABLE = SEG + 4
 
 f32 = jnp.float32
 bf16 = jnp.bfloat16
@@ -40,14 +43,38 @@
     return lax.broadcasted_iota(jnp.int32, shape, 1)
 
 
-def mirrored(value):
-    return jnp.take_along_axis(value, NY - 1 - lanes(value.shape), axis=1)
+def pick(value, index):
+    return jnp.take_along_axis(value, index, axis=1)
+
+
+def cell_at(lane):
+    return (lane % 8) * SEG + lane // 8
+
+
+def lane_of(cell):
+    return (cell % SEG) * 8 + cell // SEG
+
+
+def swept(value):
+    return pick(value, cell_at(lanes(value.shape)))
+
+
+def swept_back(value):
+    return pick(value, NY - 1 - cell_at(lanes(value.shape)))
+
+
+def restored(value):
+    return pick(value, lane_of(lanes(value.shape)))
+
+
+def restored_back(value):
+    return pick(value, lane_of(NY - 1 - lanes(value.shape)))
 
 
 def transport_kernel(
     dist, speeds_in, weights_in, collision_in, values_in, kind_in,
     out, settled_out,
-    draw, gd, fhi, flo, fac, wgt, inv_own, prod, ycoef, ascale, bscale, fxs, fys,
+    draw, gd, fhi, flo, fac, wgt, inv_own, prod, yrow, ascale, fxs, fys,
     near, far, outa, outb, rows_t, rows_p, rows_g, shp, col,
     b1, b2, b3, cbuf, crow, dpad, rhs, drive_s,
     speeds, weights, collision, wall_values, wall_kind,
@@ -63,6 +90,7 @@
     low_side = slab < 2
     partner = jnp.where(low_side, 1 - slab, 5 - slab)
     across = 3 - slab
+    beside = jnp.where(low_side, 2, 0)
 
     def device(s, x, y, z):
         return {"slab": s, "vel": (x * 2 + y) * 4 + z}
@@ -166,23 +194,43 @@
             ).wait_recv()
         return (buf[it, piece, 0] + buf[it, piece, 1]) + (buf[it, piece, 2] + buf[it, piece, 3])
 
+    def hand(it, piece, n, slot, y, s):
+        index = (y * 4 + s + 8 - slot) % 8 - 1
+        copy = pltpu.make_async_remote_copy(
+            src_ref=b3.at[it, piece, slot],
+            dst_ref=b3.at[it, piece, slot],
+            send_sem=ysend.at[it, piece, n],
+            recv_sem=yrecv.at[it, piece, index],
+            device_id=device(s, px, y, pz),
+            device_id_type=MESH,
+        )
+        copy.start()
+        return copy
+
     def spread(it, piece):
+        targets = [(1 - py, slab)]
+        for y in (py, 1 - py):
+            targets += [(y, beside), (y, beside + 1)]
+        targets.append((py, partner))
+        return [hand(it, piece, n, group, y, s) for n, (y, s) in enumerate(targets)]
+
+    def forward_far(it):
         sent = []
-        for d in range(1, 8):
-            copy = pltpu.make_async_remote_copy(
-                src_ref=b3.at[it, piece, group],
-                dst_ref=b3.at[it, piece, group],
-                send_sem=ysend.at[it, piece, d - 1],
-                recv_sem=yrecv.at[it, piece, d - 1],
-                device_id=yz[d - 1],
+        for piece in range(2):
+            source = (group + 4) % 8
+            pltpu.make_async_remote_copy(
+                src_ref=b3.at[it, piece, source],
+                dst_ref=b3.at[it, piece, source],
+                send_sem=ysend.at[it, piece, 3],
+                recv_sem=yrecv.at[it, piece, 3],
+                device_id=yz[3],
                 device_id_type=MESH,
-            )
-            copy.start()
-            sent.append(copy)
+            ).wait_recv()
+            sent.append(hand(it, piece, 6, source, py, partner))
         return sent
 
     def spread_arrived(it, piece):
-        for d in range(1, 8):
+        for d in (1, 2, 3, 5, 6, 7):
             source = (group + 8 - d) % 8
             pltpu.make_async_remote_copy(
                 src_ref=b3.at[it, piece, source],
@@ -234,8 +282,16 @@
     rate_x = jnp.abs(cx) * NX
     rate_y = jnp.abs(cy) * NY
     rows_t[0:1, :] = rate_x
-    rows_t[1:2, :] = rate_y / (1.0 + rate_y)
-    rows_t[2:3, :] = 1.0 / (1.0 + rate_y)
+    ratio = rate_y / (1.0 + rate_y)
+    powers = [ratio]
+    for _ in range(SEG - 1):
+        powers.append(powers[-1] * ratio)
+    powers.append(powers[-1] * powers[-1])
+    powers.append(powers[-1] * powers[-1])
+    powers += [zero, 1.0 / (1.0 + rate_y)]
+    for n, power in enumerate(powers):
+        for i in range(NB):
+            yrow[i, n : n + 1, :] = power[:, i * VB : (i + 1) * VB]
     rows_t[3:4, :] = jnp.where(low_side, inflow[0:1], inflow[1:2])
     rows_t[4:5, :] = fx
     rows_t[5:6, :] = fy
@@ -261,7 +317,7 @@
     lane = lanes((VB, NY))
 
     def send_out(buf, target, send, recv, it, i, to):
-        at = pl.ds(i * VB, VB)
+        at = pl.ds(i * CB, CB)
         pltpu.make_async_remote_copy(
             src_ref=buf.at[it, at],
             dst_ref=target.at[it, at],
@@ -272,7 +328,7 @@
         ).start()
 
     def wait_in(target, send, recv, it, i):
-        at = pl.ds(i * VB, VB)
+        at = pl.ds(i * CB, CB)
         pltpu.make_async_remote_copy(
             src_ref=target.at[it, at],
             dst_ref=target.at[it, at],
@@ -283,7 +339,7 @@
         ).wait_recv()
 
     def wait_out(buf, target, send, recv, it, i):
-        at = pl.ds(i * VB, VB)
+        at = pl.ds(i * CB, CB)
         pltpu.make_async_remote_copy(
             src_ref=buf.at[it, at],
             dst_ref=target.at[it, at],
@@ -293,30 +349,40 @@
             device_id_type=MESH,
         ).wait_send()
 
-    own = collision[...]
-    own_back = mirrored(jnp.concatenate([own, own], axis=0))
+    twice = jnp.concatenate([collision[...], collision[...]], axis=0)
+    own, own_back = swept(twice), swept_back(twice)
 
     def pass_on(it, i):
-        at = pl.ds(i * VB, VB)
+        at = pl.ds(i * CB, CB)
         wait_in(near, nsend, nrecv, it, i)
         outa[it, at, :] = prod[at, :] * near[it, at, :] + gd[XL - 1, at, :]
         send_out(outa, far, fsend, frecv, it, i, across)
 
-    def sweep_source(fields, at, it, i):
+    def sweep_source(fields, at):
         total = inv_own[0, at, :] * fields[0]
         gd[0, at, :] = total
         for q in range(1, XL):
             total = fac[PAD + q, at, :] * total + inv_own[q, at, :] * fields[q]
             gd[q, at, :] = total
 
+    def chain_step(it, c):
         @pl.when(edge)
         def _():
-            outa[it, at, :] = prod[at, :] * near[it, at, :] + total
-            send_out(outa, near, nsend, nrecv, it, i, partner)
-
-        @pl.when(jnp.logical_and(middle, i >= LAG))
+            at = pl.ds(c * CB, CB)
+            outa[it, at, :] = prod[at, :] * near[it, at, :] + gd[XL - 1, at, :]
+            send_out(outa, near, nsend, nrecv, it, c, partner)
+
+        @pl.when(jnp.logical_and(middle, c >= LAG))
         def _():
-            pass_on(it, i - LAG)
+            pass_on(it, c - LAG)
+
+    def in_groups(block, it):
+        def group_of(c, carry):
+            lax.fori_loop(c * (CB // VB), (c + 1) * (CB // VB), block, 0)
+            if it is not None:
+                chain_step(it, c)
+            return carry
+        lax.fori_loop(0, NC, group_of, 0)
 
     def prepare(i, c):
         at = pl.ds(i * VB, VB)
@@ -324,11 +390,6 @@
         wide = lambda k: jnp.broadcast_to(cols[:, k : k + 1], (VB, NY))
         a = wide(0)
         ascale[at, :] = a
-        power = wide(1)
-        for k, step in enumerate(STEPS):
-            ycoef[k, at, :] = jnp.where(lane >= step, power, 0.0)
-            power = power * power
-        bscale[at, :] = wide(2)
         fxv, fyv = wide(4), wide(5)
         fxs[at, :] = fxv
         fys[at, :] = fyv
@@ -339,7 +400,7 @@
             for it in range(ITERS):
                 near[it, at, :] = wide(3)
 
-        index = jnp.where(upward, lane, NY - 1 - lane)
+        index = jnp.where(upward, cell_at(lane), NY - 1 - cell_at(lane))
         product = None
         fields = []
         for q in range(XL):
@@ -358,10 +419,10 @@
             picked = jnp.where(forward, draw[q, at, :], draw[m, at, :])
             fields.append(jnp.take_along_axis(picked, index, axis=1))
         prod[at, :] = product
-        sweep_source(fields, at, 0, i)
+        sweep_source(fields, at)
         return c
 
-    lax.fori_loop(0, NB, prepare, 0)
+    in_groups(prepare, 0)
 
     def chain_across(it):
         @pl.when(middle)
@@ -369,13 +430,13 @@
             def step(i, c):
                 pass_on(it, i)
                 return c
-            lax.fori_loop(NB - LAG, NB, step, 0)
+            lax.fori_loop(NC - LAG, NC, step, 0)
 
     def chain_back(it):
         @pl.when(middle)
         def _():
             def step(i, c):
-                at = pl.ds(i * VB, VB)
+                at = pl.ds(i * CB, CB)
                 wait_in(far, fsend, frecv, it, i)
                 outb[it, at, :] = prod[at, :] * far[it, at, :] + gd[XL - 1, at, :]
                 pltpu.make_async_remote_copy(
@@ -387,7 +448,7 @@
                     device_id_type=MESH,
                 ).start()
                 return c
-            lax.fori_loop(0, NB, step, 0)
+            lax.fori_loop(0, NC, step, 0)
 
     def drain_chain(it):
         @pl.when(middle)
@@ -396,14 +457,14 @@
                 wait_out(outa, far, fsend, frecv, it, i)
                 wait_out(outb, far, nsend, frecv, it, i)
                 return c
-            lax.fori_loop(0, NB, step, 0)
+            lax.fori_loop(0, NC, step, 0)
 
         @pl.when(edge)
         def _():
             def step(i, c):
                 wait_out(outa, near, nsend, nrecv, it, i)
                 return c
-            lax.fori_loop(0, NB, step, 0)
+            lax.fori_loop(0, NC, step, 0)
 
     sent += second_stage(0)
     chain_across(0)
@@ -420,10 +481,10 @@
         ).wait_recv()
     crow[...] = jnp.zeros_like(crow)
     everywhere = jnp.concatenate([cbuf[s] for s in range(SLABS)], axis=0)
-    turned = mirrored(everywhere)
+    ahead_rows, back_rows = swept(everywhere), swept_back(everywhere)
     for i in range(NX):
-        crow[0, PAD + i] = jnp.broadcast_to(everywhere[i : i + 1], (8, NY))
-        crow[1, PAD + i] = jnp.broadcast_to(turned[i : i + 1], (8, NY))
+        for n, source in enumerate((ahead_rows, back_rows, everywhere)):
+            crow[n, PAD + i] = jnp.broadcast_to(source[i : i + 1], (8, NY))
 
     def upstream(start, stop):
         def at_cell(r, c):
@@ -452,6 +513,7 @@
     sent += third_stage(0)
     chain_back(0)
     upstream(5, PAD)
+    sent += forward_far(0)
 
     cell = lanes((8, NY))
     sub = lax.broadcasted_iota(jnp.int32, (8, NY), 0)
@@ -482,7 +544,7 @@
             right = along[i + 1] if i + 1 < NX else nothing
             left = along[i - 1] if i > 0 else nothing
             target.append(a - (0.5 * (right - left) + 0.5 * (above(cross) - below(cross))))
-            stiff = 1.0 / crow[0, PAD + i]
+            stiff = 1.0 / crow[2, PAD + i]
             kappa.append(stiff)
             down.append(1.0 / (1.0 + 4.0 * stiff))
         settled = head
@@ -498,9 +560,9 @@
         for i in range(NX):
             drive = jnp.where(sub < 5, settled[i], head[i])
             drive_s[i] = drive
-            hi, lo = split(drive)
+            hi, lo = split(swept(drive))
             dpad[0, PAD + i] = jnp.concatenate([hi, lo], axis=0)
-            hi, lo = split(mirrored(drive))
+            hi, lo = split(swept_back(drive))
             dpad[1, PAD + i] = jnp.concatenate([hi, lo], axis=0)
         for r in range(NX):
             ahead = XL * slab + r
@@ -512,8 +574,33 @@
                 rhs[g * 32 : g * 32 + 16, at] = tile
                 rhs[g * 32 + 16 : g * 32 + 32, at] = tile
 
+    segment = lax.broadcasted_iota(jnp.int32, (8, NY), 0)
+
+    def along_y(g, table):
+        columns = jnp.transpose(g)
+        ratio, scale = table[0:1], table[SEG + 3 : SEG + 4]
+        inner = []
+        for t in range(SEG):
+            h = columns[8 * t : 8 * t + 8] * scale
+            inner.append(h + ratio * inner[-1] if t else h)
+        ends = inner[-1]
+        for n, step in enumerate((1, 2, 4)):
+            moved = jnp.where(segment >= step, pltpu.roll(ends, step, 0), 0.0)
+            k = SEG - 1 + n
+            ends = ends + table[k : k + 1] * moved
+        carry = jnp.where(segment >= 1, pltpu.roll(ends, 1, 0), 0.0)
+        whole = [inner[t] + table[t : t + 1] * carry for t in range(SEG)]
+        return jnp.transpose(jnp.concatenate(whole, axis=0))
+
     def main(it):
         last = it == ITERS - 1
+
+        @pl.when(edge)
+        def _():
+            def ready(i, c):
+                wait_in(far, fsend, frecv, it, i)
+                return c
+            lax.fori_loop(0, NC, ready, 0)
 
         def block(i, c):
             at = pl.ds(i * VB, VB)
@@ -521,11 +608,6 @@
             enter = wgt[0, at, :] * eq[:, 0:NY]
             for r in range(1, PAD):
                 enter = fac[r, at, :] * enter + wgt[r, at, :] * eq[:, r * NY : (r + 1) * NY]
-
-            @pl.when(edge)
-            def _():
-                wait_in(far, fsend, frecv, it, i)
-
             forward = fxs[at, :] > 0.5
             from_near = jnp.where(low_side, fxs[at, :], 1.0 - fxs[at, :]) > 0.5
             enter = enter + jnp.where(from_near, near[it, at, :], far[it, at, :])
@@ -533,26 +615,24 @@
             for q in range(XL):
                 r = PAD + q
                 enter = fac[r, at, :] * enter + wgt[r, at, :] * eq[:, r * NY : (r + 1) * NY]
-                h = (gd[q, at, :] + enter) * bscale[at, :]
-                for k, step in enumerate(STEPS):
-                    h = h + ycoef[k, at, :] * pltpu.roll(h, step, 1)
+                h = along_y(gd[q, at, :] + enter, yrow[i])
                 fields.append(h)
                 if not last:
                     hi, lo = split(h)
                     fhi[at, q * NY : (q + 1) * NY] = hi
                     flo[at, q * NY : (q + 1) * NY] = lo
             if last:
-                index = jnp.where(fys[at, :] > 0.5, lane, NY - 1 - lane)
+                index = jnp.where(fys[at, :] > 0.5, lane_of(lane), lane_of(NY - 1 - lane))
                 for x in range(XL):
                     picked = jnp.where(forward, fields[x], fields[XL - 1 - x])
                     out[pl.ds(i * VB * XL + x, VB, stride=XL), :] = jnp.take_along_axis(
                         picked, index, axis=1
                     )
             else:
-                sweep_source(fields, at, it + 1, i)
+                sweep_source(fields, at)
             return c
 
-        lax.fori_loop(0, NB, block, 0)
+        in_groups(block, None if last else it + 1)
 
     for it in range(ITERS):
         macro(it)
@@ -565,14 +645,16 @@
             )
             up = groups[0:KR] + turn(groups[2 * KR : 3 * KR])
             down = groups[KR : 2 * KR] + turn(groups[3 * KR : 4 * KR])
-            moment = up + jnp.concatenate(
-                [mirrored(down[:, x * NY : (x + 1) * NY]) for x in range(XL)], axis=1
+            spans = [slice(x * NY, (x + 1) * NY) for x in range(XL)]
+            moment = jnp.concatenate(
+                [restored(up[:, at]) + restored_back(down[:, at]) for at in spans], axis=1
             )
             sent += start_reduce(it + 1, moment)
             chain_across(it + 1)
             sent += second_stage(it + 1)
             chain_back(it + 1)
             sent += third_stage(it + 1)
+            sent += forward_far(it + 1)
 
     for x in range(XL):
         settled_out[:, x, :] = drive_s[XL * slab + x][0:5]
@@ -597,8 +679,7 @@
         pltpu.VMEM((NX, *full), f32),
         pltpu.VMEM((XL, *full), f32),
         pltpu.VMEM(full, f32),
-        pltpu.VMEM((len(STEPS), *full), f32),
-        pltpu.VMEM(full, f32),
+        pltpu.VMEM((NB, TABLE, VB), f32),
         pltpu.VMEM(full, f32),
         pltpu.VMEM(full, f32),
         pltpu.VMEM(full, f32),
@@ -615,7 +696,7 @@
         pltpu.VMEM((ITERS, 2, 4, ROWS, HALF), f32),
         pltpu.VMEM((ITERS, 2, 8, ROWS, HALF), f32),
         pltpu.VMEM((SLABS, XL, NY), f32),
-        pltpu.VMEM((2, NX + 2 * PAD, 8, NY), f32),
+        pltpu.VMEM((3, NX + 2 * PAD, 8, NY), f32),
         pltpu.VMEM((2, NX + 2 * PAD, 16, NY), bf16),
         pltpu.VMEM((128, NX * NY), bf16),
         pltpu.VMEM((NX, 8, NY), f32),
@@ -632,10 +713,10 @@
         dma((ITERS, 2, 7)),
         dma((3,)),
         dma((3,)),
-        dma((ITERS, NB)),
-        dma((ITERS, NB)),
-        dma((ITERS, NB)),
-        dma((ITERS, NB)),
+        dma((ITERS, NC)),
+        dma((ITERS, NC)),
+        dma((ITERS, NC)),
+        dma((ITERS, NC)),
     ]
     rows, settled = pl.pallas_call(
         transport_kernel,

time: 51.5 us -> 45.9 us (0.89)
  Pallas kernels: 49 us -> 43.4 us
    pallas_call x1, Pallas kernels: 49 us -> 43.4 us  [on_device(): pl.pallas_call(transport_kernel, out_shape=(jax.ShapeDtypeStruct((V * XL,...]
where the time goes in v3:
time: 45.9 us; the launch traced here: 45.8 us
  Pallas kernels  43.4 us (95%)
  local copies, waits for them, and re-layouts  1.74 us (4%)
  between operations  0.64 us (1%)
    pallas_call x1, Pallas kernels, on_device(): pl.pallas_call(transport_kernel, out_shape=(jax.ShapeDtypeStruct((V * XL,...  43.4 us
    unnamed x2, local copies, waits for them, and re-layouts  1.74 us

profile of v3, /device:TPU:1, one launch (start us, length us, event | category | flops | bytes accessed | tf_op | source)
XLA Modules:
  0.0 45.8 jit_solution(8488990209438224403)
XLA Ops:
  0.6 43.4 %transport.1 = (f32[3072,128]{1,0:T(8,128)S(1)}, f32[5,4,128]{2,1,0:T(4,128)S(1)}) custom-call(f32[768,4,128]{2,1,0:T(4,128)} %dist.1, f32[3,768]{1,0:T(4,128)} %speeds_in.1, f32[768]{0:T(1024)} %weights_in.1, f32[4,128]{1,0:T(4,128)} %collision_in.1, f32[2,768]{1,0:T(2,128)} %values_in.1, s32[2,768]{1,0:T(2,128)} %kind_in.1), custom_call_target="tpu_custom_call" | custom-call | tf_op jit(solution)/shard_map/transport/pallas_call | solution.py:721
  44.0 1.1 %copy.10 = f32[768,4,128]{2,1,0:T(4,128)} copy(f32[768,4,128]{2,1,0:T(4,128)S(1)} %bitcast.1) | data formatting | bytes 3145728
  45.2 0.6 %copy.11 = f32[5,4,128]{2,1,0:T(4,128)} copy(f32[5,4,128]{2,1,0:T(4,128)S(1)} %get-tuple-element.9) | data formatting | bytes 20480

commit v4 on v3

--- a/solution.py
+++ b/solution.py
@@ -96,7 +96,10 @@
         return {"slab": s, "vel": (x * 2 + y) * 4 + z}
 
     loads = [
-        pltpu.make_async_copy(dist.at[:, x, :], draw.at[x], dsem.at[x]) for x in range(XL)
+        pltpu.make_async_copy(
+            dist.at[pl.ds(i * VB * XL, VB * XL)], draw.at[pl.ds(i * VB * XL, VB * XL)], dsem.at[i]
+        )
+        for i in range(NB)
     ]
     small = [
         pltpu.make_async_copy(source, target, ssem.at[n])
@@ -148,15 +151,17 @@
         rows_g[g * KR : (g + 1) * KR, :] = rows_hi * m
         rows_g[4 * KR + g * KR : 4 * KR + (g + 1) * KR, :] = rows_lo * m
 
-    for x in range(XL):
-        loads[x].wait()
-        def cast(i, c, x=x):
-            at = pl.ds(i * VB, VB)
-            hi, lo = split(draw[x, at, :])
+    def cast(i, c):
+        at = pl.ds(i * VB, VB)
+        rows_at = pl.ds(i * VB * XL, VB * XL)
+        pltpu.make_async_copy(dist.at[rows_at], draw.at[rows_at], dsem.at[i]).wait()
+        for x in range(XL):
+            hi, lo = split(draw[pl.ds(i * VB * XL + x, VB, stride=XL), :])
             fhi[at, x * NY : (x + 1) * NY] = hi
             flo[at, x * NY : (x + 1) * NY] = lo
-            return c
-        lax.fori_loop(0, NB, cast, 0)
+        return c
+
+    lax.fori_loop(0, NB, cast, 0)
     first = dot(rows_p[...], fhi[...])
     moment = first[0:KR] + first[KR : 2 * KR] + dot(rows_p[0:KR, :], flo[...])
 
@@ -378,7 +383,8 @@
 
     def in_groups(block, it):
         def group_of(c, carry):
-            lax.fori_loop(c * (CB // VB), (c + 1) * (CB // VB), block, 0)
+            for n in range(CB // VB):
+                block(c * (CB // VB) + n, 0)
             if it is not None:
                 chain_step(it, c)
             return carry
@@ -416,7 +422,11 @@
             fac[PAD + q, at, :] = f
             wgt[PAD + q, at, :] = rate * inv
             product = f if product is None else product * f
-            picked = jnp.where(forward, draw[q, at, :], draw[m, at, :])
+            picked = jnp.where(
+                forward,
+                draw[pl.ds(i * VB * XL + q, VB, stride=XL), :],
+                draw[pl.ds(i * VB * XL + m, VB, stride=XL), :],
+            )
             fields.append(jnp.take_along_axis(picked, index, axis=1))
         prod[at, :] = product
         sweep_source(fields, at)
@@ -655,14 +665,13 @@
             chain_back(it + 1)
             sent += third_stage(it + 1)
             sent += forward_far(it + 1)
+            for done in range(ITERS):
+                drain_chain(done)
+            for copy in sent:
+                copy.wait_send()
 
     for x in range(XL):
         settled_out[:, x, :] = drive_s[XL * slab + x][0:5]
-
-    for it in range(ITERS):
-        drain_chain(it)
-    for copy in sent:
-        copy.wait_send()
 
 
 def on_device(dist, speeds, weights, collision, wall_values, wall_kind):
@@ -671,7 +680,7 @@
     dma = pltpu.SemaphoreType.DMA
     full = (V, NY)
     scratch = [
-        pltpu.VMEM((XL, *full), f32),
+        pltpu.VMEM((V * XL, NY), f32),
         pltpu.VMEM((XL, *full), f32),
         pltpu.VMEM((V, XL * NY), bf16),
         pltpu.VMEM((V, XL * NY), bf16),
@@ -705,7 +714,7 @@
         pltpu.VMEM((XL, NY), f32),
         pltpu.VMEM((2, V), f32),
         pltpu.VMEM((2, V), jnp.int32),
-        dma((XL,)),
+        dma((NB,)),
         dma((5,)),
         dma((ITERS, 2, 2, 3)),
         dma((ITERS, 2, 2, 3)),
@@ -733,7 +742,7 @@
         name="transport",
     )(*(
         pltpu.with_memory_space_constraint(value, pltpu.HBM)
-        for value in (dist, speeds, weights, collision, wall_values, wall_kind)
+        for value in (dist.reshape(V * XL, NY), speeds, weights, collision, wall_values, wall_kind)
     ))
     return rows.reshape(V, XL, NY), settled
 

time: 45.9 us -> 43.5 us (0.948)
  Pallas kernels: 43.4 us -> 41 us
    pallas_call x1, Pallas kernels: 43.4 us -> 41 us  [on_device(): pl.pallas_call(transport_kernel, out_shape=(jax.ShapeDtypeStruct((V * XL,...]
where the time goes in v4:
time: 43.5 us; the launch traced here: 43.3 us
  Pallas kernels  41 us (94%)
  local copies, waits for them, and re-layouts  1.74 us (4%)
  between operations  0.64 us (1%)
    pallas_call x1, Pallas kernels, on_device(): pl.pallas_call(transport_kernel, out_shape=(jax.ShapeDtypeStruct((V * XL,...  41 us
    unnamed x2, local copies, waits for them, and re-layouts  1.74 us

profile of v4, /device:TPU:1, one launch (start us, length us, event | category | flops | bytes accessed | tf_op | source)
XLA Modules:
  0.0 43.3 jit_solution(16263199739482382491)
XLA Ops:
  0.6 41.0 %transport.1 = (f32[3072,128]{1,0:T(8,128)S(1)}, f32[5,4,128]{2,1,0:T(4,128)S(1)}) custom-call(f32[3072,128]{1,0:T(8,128)} %bitcast.3, f32[3,768]{1,0:T(4,128)} %speeds_in.1, f32[768]{0:T(1024)} %weights_in.1, f32[4,128]{1,0:T(4,128)} %collision_in.1, f32[2,768]{1,0:T(2,128)} %values_in.1, s32[2,768]{1,0:T(2,128)} %kind_in.1), custom_call_target="tpu_custom_call" | custom-call | tf_op jit(solution)/shard_map/transport/pallas_call | solution.py:730
  41.6 1.1 %copy.10 = f32[768,4,128]{2,1,0:T(4,128)} copy(f32[768,4,128]{2,1,0:T(4,128)S(1)} %bitcast.2) | data formatting | bytes 3145728
  42.7 0.6 %copy.11 = f32[5,4,128]{2,1,0:T(4,128)} copy(f32[5,4,128]{2,1,0:T(4,128)S(1)} %get-tuple-element.9) | data formatting | bytes 20480

commit v5 on v4

--- a/solution.py
+++ b/solution.py
@@ -74,7 +74,7 @@
 def transport_kernel(
     dist, speeds_in, weights_in, collision_in, values_in, kind_in,
     out, settled_out,
-    draw, gd, fhi, flo, fac, wgt, inv_own, prod, yrow, ascale, fxs, fys,
+    draw, gd, fhi, flo, fac, wgt, inv_own, prod, yrow, ascale, run, kappa_s, down_s, fxs, fys,
     near, far, outa, outb, rows_t, rows_p, rows_g, shp, col,
     b1, b2, b3, cbuf, crow, dpad, rhs, drive_s,
     speeds, weights, collision, wall_values, wall_kind,
@@ -367,7 +367,7 @@
         total = inv_own[0, at, :] * fields[0]
         gd[0, at, :] = total
         for q in range(1, XL):
-            total = fac[PAD + q, at, :] * total + inv_own[q, at, :] * fields[q]
+            total = fac[q, at, :] * total + inv_own[q, at, :] * fields[q]
             gd[q, at, :] = total
 
     def chain_step(it, c):
@@ -396,6 +396,7 @@
         wide = lambda k: jnp.broadcast_to(cols[:, k : k + 1], (VB, NY))
         a = wide(0)
         ascale[at, :] = a
+        run[at, :] = jnp.ones_like(a)
         fxv, fyv = wide(4), wide(5)
         fxs[at, :] = fxv
         fys[at, :] = fyv
@@ -419,7 +420,7 @@
             inv = 1.0 / (1.0 + a + rate)
             f = a * inv
             inv_own[q, at, :] = inv
-            fac[PAD + q, at, :] = f
+            fac[q, at, :] = f
             wgt[PAD + q, at, :] = rate * inv
             product = f if product is None else product * f
             picked = jnp.where(
@@ -495,9 +496,15 @@
     for i in range(NX):
         for n, source in enumerate((ahead_rows, back_rows, everywhere)):
             crow[n, PAD + i] = jnp.broadcast_to(source[i : i + 1], (8, NY))
+    dpad[...] = jnp.zeros_like(dpad)
+    for i in range(NX):
+        stiff = 1.0 / crow[2, PAD + i]
+        kappa_s[i] = stiff
+        down_s[i] = 1.0 / (1.0 + 4.0 * stiff)
 
     def upstream(start, stop):
-        def at_cell(r, c):
+        def at_cell(n, c):
+            r = PAD - 1 - n
             ahead = XL * slab + r
             behind = XL * slab + PAD + NX - 1 - r
             c_ff = crow[0, ahead][0:1]
@@ -512,8 +519,9 @@
                     forward, jnp.where(upward, c_ff, c_fb), jnp.where(upward, c_bf, c_bb)
                 )
                 inv = 1.0 / (1.0 + a + rate)
-                fac[r, at, :] = a * inv
-                wgt[r, at, :] = rate * inv
+                through = run[at, :]
+                wgt[r, at, :] = rate * inv * through
+                run[at, :] = a * inv * through
                 return c
             lax.fori_loop(0, NB, block, 0)
             return c
@@ -554,9 +562,8 @@
             right = along[i + 1] if i + 1 < NX else nothing
             left = along[i - 1] if i > 0 else nothing
             target.append(a - (0.5 * (right - left) + 0.5 * (above(cross) - below(cross))))
-            stiff = 1.0 / crow[2, PAD + i]
-            kappa.append(stiff)
-            down.append(1.0 / (1.0 + 4.0 * stiff))
+            kappa.append(kappa_s[i])
+            down.append(down_s[i])
         settled = head
         for _ in range(JACOBI):
             after = []
@@ -566,7 +573,6 @@
                 around = right + left + above(settled[i]) + below(settled[i])
                 after.append((target[i] + kappa[i] * around) * down[i])
             settled = after
-        dpad[...] = jnp.zeros_like(dpad)
         for i in range(NX):
             drive = jnp.where(sub < 5, settled[i], head[i])
             drive_s[i] = drive
@@ -617,14 +623,14 @@
             eq = dot(shp[at, :], rhs[...])
             enter = wgt[0, at, :] * eq[:, 0:NY]
             for r in range(1, PAD):
-                enter = fac[r, at, :] * enter + wgt[r, at, :] * eq[:, r * NY : (r + 1) * NY]
+                enter = enter + wgt[r, at, :] * eq[:, r * NY : (r + 1) * NY]
             forward = fxs[at, :] > 0.5
             from_near = jnp.where(low_side, fxs[at, :], 1.0 - fxs[at, :]) > 0.5
             enter = enter + jnp.where(from_near, near[it, at, :], far[it, at, :])
             fields = []
             for q in range(XL):
                 r = PAD + q
-                enter = fac[r, at, :] * enter + wgt[r, at, :] * eq[:, r * NY : (r + 1) * NY]
+                enter = fac[q, at, :] * enter + wgt[r, at, :] * eq[:, r * NY : (r + 1) * NY]
                 h = along_y(gd[q, at, :] + enter, yrow[i])
                 fields.append(h)
                 if not last:
@@ -674,6 +680,17 @@
         settled_out[:, x, :] = drive_s[XL * slab + x][0:5]
 
 
+def copy_out(rows, settled, rows_out, settled_out, sem):
+    copies = [
+        pltpu.make_async_copy(settled, settled_out, sem.at[0]),
+        pltpu.make_async_copy(rows, rows_out, sem.at[1]),
+    ]
+    for copy in copies:
+        copy.start()
+    for copy in copies:
+        copy.wait()
+
+
 def on_device(dist, speeds, weights, collision, wall_values, wall_kind):
     vmem = pl.BlockSpec(memory_space=pltpu.VMEM)
     hbm = pl.BlockSpec(memory_space=pltpu.HBM)
@@ -684,12 +701,15 @@
         pltpu.VMEM((XL, *full), f32),
         pltpu.VMEM((V, XL * NY), bf16),
         pltpu.VMEM((V, XL * NY), bf16),
-        pltpu.VMEM((NX, *full), f32),
+        pltpu.VMEM((XL, *full), f32),
         pltpu.VMEM((NX, *full), f32),
         pltpu.VMEM((XL, *full), f32),
         pltpu.VMEM(full, f32),
         pltpu.VMEM((NB, TABLE, VB), f32),
         pltpu.VMEM(full, f32),
+        pltpu.VMEM(full, f32),
+        pltpu.VMEM((NX, 8, NY), f32),
+        pltpu.VMEM((NX, 8, NY), f32),
         pltpu.VMEM(full, f32),
         pltpu.VMEM(full, f32),
         pltpu.VMEM((ITERS, *full), f32),
@@ -744,6 +764,19 @@
         pltpu.with_memory_space_constraint(value, pltpu.HBM)
         for value in (dist.reshape(V * XL, NY), speeds, weights, collision, wall_values, wall_kind)
     ))
+    anywhere = pl.BlockSpec(memory_space=pl.ANY)
+    rows, settled = pl.pallas_call(
+        copy_out,
+        out_shape=(
+            jax.ShapeDtypeStruct((V * XL, NY), f32),
+            jax.ShapeDtypeStruct((5, XL, NY), f32),
+        ),
+        in_specs=[anywhere, anywhere],
+        out_specs=(hbm, hbm),
+        scratch_shapes=[dma((2,))],
+        compiler_params=pltpu.CompilerParams(vmem_limit_bytes=1024 * 1024),
+        name="copy_out",
+    )(rows, settled)
     return rows.reshape(V, XL, NY), settled
 
 

time: 43.5 us -> 42.8 us (0.984)
  local copies, waits for them, and re-layouts: 1.74 us -> 0 us
  Pallas kernels: 41 us -> 42 us
    unnamed x2 -> x0, local copies, waits for them, and re-layouts: 1.74 us -> none
    pallas_call x0 -> x1, Pallas kernels: none -> 1.17 us  [on_device(): pl.pallas_call(copy_out, out_shape=(jax.ShapeDtypeStruct((V * XL, NY), f3...]
where the time goes in v5:
time: 42.8 us; the launch traced here: 42.7 us
  Pallas kernels  42 us (98%)
  between operations  0.64 us (1%)
    pallas_call x1, Pallas kernels, on_device(): pl.pallas_call(transport_kernel, out_shape=(jax.ShapeDtypeStruct((V * XL,...  40.9 us
    pallas_call x1, Pallas kernels, on_device(): pl.pallas_call(copy_out, out_shape=(jax.ShapeDtypeStruct((V * XL, NY), f3...  1.17 us

profile of v5, /device:TPU:1, one launch (start us, length us, event | category | flops | bytes accessed | tf_op | source)
XLA Modules:
  0.0 42.7 jit_solution(3994368379751124570)
XLA Ops:
  0.6 40.9 %transport.1 = (f32[3072,128]{1,0:T(8,128)S(1)}, f32[5,4,128]{2,1,0:T(4,128)S(1)}) custom-call(f32[3072,128]{1,0:T(8,128)} %bitcast.2, f32[3,768]{1,0:T(4,128)} %speeds_in.1, f32[768]{0:T(1024)} %weights_in.1, f32[4,128]{1,0:T(4,128)} %collision_in.1, f32[2,768]{1,0:T(2,128)} %values_in.1, s32[2,768]{1,0:T(2,128)} %kind_in.1), custom_call_target="tpu_custom_call" | custom-call | tf_op jit(solution)/shard_map/transport/pallas_call | solution.py:750
  41.5 1.2 %copy_out.1 = (f32[3072,128]{1,0:T(8,128)}, f32[5,4,128]{2,1,0:T(4,128)}) custom-call(f32[3072,128]{1,0:T(8,128)S(1)} %get-tuple-element.6.rows, f32[5,4,128]{2,1,0:T(4,128)S(1)} %get-tuple-element.7.settled), custom_call_target="tpu_custom_call" | custom-call | tf_op jit(solution)/shard_map/copy_out/pallas_call | solution.py:768

commit v6 on v5

--- a/solution.py
+++ b/solution.py
@@ -172,7 +172,7 @@
     def exchange(buf, stage, it, piece):
         me, to = axes[(stage + piece) % 2]
         sent = []
-        for d in range(1, 4):
+        for d in (2, 1, 3):
             copy = pltpu.make_async_remote_copy(
                 src_ref=buf.at[it, piece, me],
                 dst_ref=buf.at[it, piece, me],
@@ -213,11 +213,11 @@
         return copy
 
     def spread(it, piece):
-        targets = [(1 - py, slab)]
+        targets = []
         for y in (py, 1 - py):
             targets += [(y, beside), (y, beside + 1)]
         targets.append((py, partner))
-        return [hand(it, piece, n, group, y, s) for n, (y, s) in enumerate(targets)]
+        return [hand(it, piece, n + 1, group, y, s) for n, (y, s) in enumerate(targets)]
 
     def forward_far(it):
         sent = []
@@ -265,6 +265,8 @@
         sent = []
         for piece in range(2):
             b3[it, piece, group] = arrived(b2, 1, it, piece)
+            sent.append(hand(it, piece, 0, group, 1 - py, slab))
+        for piece in range(2):
             sent += spread(it, piece)
         return sent
 

time: 42.8 us -> 42.4 us (level)
    pallas_call x1, Pallas kernels: 40.9 us -> 40.4 us  [on_device(): pl.pallas_call(transport_kernel, out_shape=(jax.ShapeDtypeStruct((V * XL,...]
where the time goes in v6:
time: 42.4 us; the launch traced here: 42.2 us
  Pallas kernels  41.6 us (98%)
  between operations  0.64 us (2%)
    pallas_call x1, Pallas kernels, on_device(): pl.pallas_call(transport_kernel, out_shape=(jax.ShapeDtypeStruct((V * XL,...  40.4 us
    pallas_call x1, Pallas kernels, on_device(): pl.pallas_call(copy_out, out_shape=(jax.ShapeDtypeStruct((V * XL, NY), f3...  1.17 us

profile of v6, /device:TPU:1, one launch (start us, length us, event | category | flops | bytes accessed | tf_op | source)
XLA Modules:
  0.0 42.2 jit_solution(1133493688898121415)
XLA Ops:
  0.6 40.4 %transport.1 = (f32[3072,128]{1,0:T(8,128)S(1)}, f32[5,4,128]{2,1,0:T(4,128)S(1)}) custom-call(f32[3072,128]{1,0:T(8,128)} %bitcast.2, f32[3,768]{1,0:T(4,128)} %speeds_in.1, f32[768]{0:T(1024)} %weights_in.1, f32[4,128]{1,0:T(4,128)} %collision_in.1, f32[2,768]{1,0:T(2,128)} %values_in.1, s32[2,768]{1,0:T(2,128)} %kind_in.1), custom_call_target="tpu_custom_call" | custom-call | tf_op jit(solution)/shard_map/transport/pallas_call | solution.py:752
  41.1 1.2 %copy_out.1 = (f32[3072,128]{1,0:T(8,128)}, f32[5,4,128]{2,1,0:T(4,128)}) custom-call(f32[3072,128]{1,0:T(8,128)S(1)} %get-tuple-element.6.rows, f32[5,4,128]{2,1,0:T(4,128)S(1)} %get-tuple-element.7.settled), custom_call_target="tpu_custom_call" | custom-call | tf_op jit(solution)/shard_map/copy_out/pallas_call | solution.py:770

commit v7 on v6

--- a/solution.py
+++ b/solution.py
@@ -529,11 +529,12 @@
             return c
         lax.fori_loop(start, stop, at_cell, 0)
 
-    upstream(0, 5)
+    upstream(0, 4)
     sent += third_stage(0)
     chain_back(0)
-    upstream(5, PAD)
+    upstream(4, 9)
     sent += forward_far(0)
+    upstream(9, PAD)
 
     cell = lanes((8, NY))
     sub = lax.broadcasted_iota(jnp.int32, (8, NY), 0)

time: 42.4 us -> 41.9 us (0.988)
    pallas_call x1, Pallas kernels: 40.4 us -> 40 us  [on_device(): pl.pallas_call(transport_kernel, out_shape=(jax.ShapeDtypeStruct((V * XL,...]
where the time goes in v7:
time: 41.9 us; the launch traced here: 41.8 us
  Pallas kernels  41.2 us (98%)
  between operations  0.64 us (2%)
    pallas_call x1, Pallas kernels, on_device(): pl.pallas_call(transport_kernel, out_shape=(jax.ShapeDtypeStruct((V * XL,...  40 us
    pallas_call x1, Pallas kernels, on_device(): pl.pallas_call(copy_out, out_shape=(jax.ShapeDtypeStruct((V * XL, NY), f3...  1.17 us

profile of v7, /device:TPU:1, one launch (start us, length us, event | category | flops | bytes accessed | tf_op | source)
XLA Modules:
  0.0 41.8 jit_solution(8894029060039190251)
XLA Ops:
  0.6 40.0 %transport.1 = (f32[3072,128]{1,0:T(8,128)S(1)}, f32[5,4,128]{2,1,0:T(4,128)S(1)}) custom-call(f32[3072,128]{1,0:T(8,128)} %bitcast.2, f32[3,768]{1,0:T(4,128)} %speeds_in.1, f32[768]{0:T(1024)} %weights_in.1, f32[4,128]{1,0:T(4,128)} %collision_in.1, f32[2,768]{1,0:T(2,128)} %values_in.1, s32[2,768]{1,0:T(2,128)} %kind_in.1), custom_call_target="tpu_custom_call" | custom-call | tf_op jit(solution)/shard_map/transport/pallas_call | solution.py:753
  40.6 1.2 %copy_out.1 = (f32[3072,128]{1,0:T(8,128)}, f32[5,4,128]{2,1,0:T(4,128)}) custom-call(f32[3072,128]{1,0:T(8,128)S(1)} %get-tuple-element.6.rows, f32[5,4,128]{2,1,0:T(4,128)S(1)} %get-tuple-element.7.settled), custom_call_target="tpu_custom_call" | custom-call | tf_op jit(solution)/shard_map/copy_out/pallas_call | solution.py:771
